TPU v7x, 256 devices: a whole 4x4x8 slice. The times are simulated.
256 devices in a mesh: gy: 4 (over z_hi), gx: 64 (over y, x, z_lo, core).
Axes of the slice: x: 4, y: 4, z: 8 (z_hi: 4, z_lo: 2; z = z_hi * 2 + z_lo), core: 2. Of those that a mesh axis runs over, the one named last changes fastest.
Arguments:
- inputs: bfloat16 [128, 4096, 256], P('gy', 'gx'), may hold values from -6 to 6
- cotangent: bfloat16 [128, 4096, 256], P('gy', 'gx'), may hold values from -6 to 6
- mode_weight: bfloat16 [2, 32, 256, 256], P(None, None, 'gx'), may hold values from -2.09375 to 2.09375
- w_in: bfloat16 [256, 1024], replicated, may hold values from -0.375 to 0.375
- w_out: bfloat16 [1024, 256], replicated, may hold values from -0.1875 to 0.1875
Outputs:
- d_inputs: bfloat16 [128, 4096, 256], P('gy', 'gx')
- d_mode: float32 [2, 32, 256, 256], P(None, 'gy', 'gx')
- d_w_in: float32 [256, 1024], P(None, ('gy', 'gx'))
- d_w_out: float32 [1024, 256], P(('gy', 'gx'))
All inputs are finite; a program needn't handle non-finite values.
Results may differ from a plain program's by a relative error of at most 0.014.
Values may be sent and summed in bfloat16 or wider, within the bound.
No kernel may reach another device: no remote copies, remote signals or barrier semaphores. Data moves between devices by JAX's collectives and lax.ppermute only.
A program may use at most 64 MiB of HBM per device.

v0:
```python
import math

import jax
import jax.numpy as jnp
from jax import lax
from jax.sharding import PartitionSpec as P

M = 32


def bases(positions, length, modes):
    order = jnp.arange(modes, dtype=jnp.int32)
    phase = positions[:, None] * order[None, :] % length
    angle = phase.astype(jnp.float32) * (2.0 * math.pi / length)
    factor = 1.0 / math.sqrt(length)
    cosine = jnp.cos(angle) * factor
    sine = jnp.sin(angle) * factor
    forward = jnp.concatenate([cosine, -sine], axis=1).astype(jnp.bfloat16)
    weight = jnp.where(order == 0, 1.0, 2.0).astype(jnp.float32)
    inverse = jnp.concatenate([cosine * weight, -sine * weight], axis=1).T.astype(jnp.bfloat16)
    return (forward, inverse)


def smooth_gate(values):
    return jax.nn.gelu(values, approximate=True)


def contract(form, left, right):
    return jnp.einsum(form, left, right, preferred_element_type=jnp.float32)


def local(inputs, cotangent, mode_weight, w_in, w_out):
    line_count, col_count, chan_count = inputs.shape
    x_devices = lax.axis_size("gx")
    y_devices = lax.axis_size("gy")
    own_rows = chan_count // x_devices
    total_x = col_count * x_devices
    positions = lax.axis_index("gx") * col_count + jnp.arange(col_count, dtype=jnp.int32)
    forward, inverse = bases(positions, total_x, M)
    width = 2 * M * line_count
    w_re = mode_weight[0]
    w_im = mode_weight[1]
    piece = inputs
    spectrum = lax.psum_scatter(
        contract("yxc,xm->cmy", piece, forward).reshape(lax.axis_size("gx") * own_rows, width),
        "gx",
        scatter_dimension=0,
        tiled=True,
    ).astype(jnp.bfloat16)
    spectrum = spectrum.reshape(own_rows, 2, M, line_count)
    own_re = spectrum[:, 0]
    own_im = spectrum[:, 1]
    vr = contract("cky,kco->oky", own_re, w_re) - contract("cky,kco->oky", own_im, w_im)
    vi = contract("cky,kco->oky", own_re, w_im) + contract("cky,kco->oky", own_im, w_re)
    mixed = lax.psum(jnp.stack([vr, vi], axis=1).reshape(chan_count, width), "gx").astype(
        jnp.bfloat16
    )
    mixed = mixed.reshape(chan_count, 2 * M, line_count)
    hidden = contract("omy,mx->yxo", mixed, inverse).astype(jnp.bfloat16)
    point_rows = line_count * col_count
    flat_h = hidden.reshape(point_rows, chan_count)
    flat_g = cotangent.reshape(point_rows, chan_count)
    pre = jnp.dot(flat_h, w_in, preferred_element_type=jnp.float32)
    act, pullback = jax.vjp(smooth_gate, pre)
    act = act.astype(jnp.bfloat16)
    grad_out = jnp.dot(act.T, flat_g, preferred_element_type=jnp.float32)
    grad_act = jnp.dot(flat_g, w_out.T, preferred_element_type=jnp.float32)
    d_pre = pullback(grad_act)[0].astype(jnp.bfloat16)
    grad_in = jnp.dot(flat_h.T, d_pre, preferred_element_type=jnp.float32)
    d_hidden = jnp.dot(d_pre, w_in.T, preferred_element_type=jnp.float32).astype(jnp.bfloat16)
    d_hidden = d_hidden.reshape(line_count, col_count, chan_count)
    piece = d_hidden
    d_mixed = lax.psum(
        contract("yxo,mx->omy", piece, inverse).reshape(chan_count, width), "gx"
    ).astype(jnp.bfloat16)
    d_mixed = d_mixed.reshape(chan_count, 2, M, line_count)
    dv_re = d_mixed[:, 0]
    dv_im = d_mixed[:, 1]
    g_re = contract("cky,oky->kco", own_re, dv_re) + contract("cky,oky->kco", own_im, dv_im)
    g_im = contract("cky,oky->kco", own_re, dv_im) - contract("cky,oky->kco", own_im, dv_re)
    mode_grad = jnp.stack([g_re, g_im], axis=0)
    du_re = contract("kco,oky->cky", w_re, dv_re) + contract("kco,oky->cky", w_im, dv_im)
    du_im = contract("kco,oky->cky", w_re, dv_im) - contract("kco,oky->cky", w_im, dv_re)
    coef_local = jnp.stack([du_re, du_im], axis=1).astype(jnp.bfloat16).reshape(own_rows, width)
    coef_all = lax.all_gather(coef_local, "gx", axis=0, tiled=True)
    coef_all = coef_all.reshape(chan_count, 2 * M, line_count)
    returned = contract("cmy,xm->yxc", coef_all, forward)
    d_inputs = (cotangent.astype(jnp.float32) + returned).astype(jnp.bfloat16)
    sum_in, sum_out = (
        lax.psum_scatter(grad_in, ("gy", "gx"), scatter_dimension=1, tiled=True),
        lax.psum_scatter(grad_out, ("gy", "gx"), scatter_dimension=0, tiled=True),
    )
    mode_sum = lax.psum_scatter(
        mode_grad.astype(jnp.bfloat16), "gy", scatter_dimension=1, tiled=True
    ).astype(jnp.float32)
    total_lines = line_count * y_devices
    scale_mlp = 1.0 / math.sqrt(total_lines * total_x)
    scale_mode = 1.0 / math.sqrt(total_lines)
    return (d_inputs, mode_sum * scale_mode, sum_in * scale_mlp, sum_out * scale_mlp)


def solution(mesh):
    placed = (P("gy", "gx", None), P("gy", "gx", None), P(None, None, "gx", None), P(), P())
    return jax.shard_map(
        local,
        mesh=mesh,
        in_specs=placed,
        out_specs=(
            P("gy", "gx", None),
            P(None, "gy", "gx", None),
            P(None, ("gy", "gx")),
            P(("gy", "gx"), None),
        ),
        check_vma=False,
    )
```

profile of v0, /device:TPU:2, one launch (start us, length us, event | category | flops | bytes accessed | tf_op | source)
XLA Modules:
  0.0 1225.8 jit_solution(1058535939683119290)
XLA Ops:
  8.0 0.0 reduce-scatter.6.cloned.1.call-start
  8.1 0.1 multiply_convert_fusion.3
  8.2 1.0 copy-done
  9.2 0.4 convolution_bitcast_fusion.1
  9.7 1.2 copy.31
  10.9 290.5 %all-reduce.10 = bf16[256,2048]{0,1:T(8,128)(2,1)} all-reduce(f32[256,2048]{0,1:T(8,128)S(1)} %bitcast.124), channel_id=2, replica_groups=mesh['gy'=4,'gx'=64] {'gx'}, use_global_device_ids=true, to_apply=%region_0.1.clone | all-reduce | flops 524288 | bytes 3145728
  301.4 0.6 dynamic-slice
  302.6 1.3 dynamic-slice_convert_fusion
  303.9 0.3 copy.67
  304.2 1.2 fusion.26
  305.4 1.2 fusion.32
  306.6 0.3 copy.68
  306.9 1.2 fusion.9
  308.2 1.2 fusion.10
  309.4 0.1 pad_maximum_fusion
  309.5 296.2 %all-reduce.11 = bf16[256,2048]{0,1:T(8,128)(2,1)} all-reduce(f32[256,2048]{0,1:T(8,128)S(1)} %bitcast.123), channel_id=1, replica_groups=mesh['gy'=4,'gx'=64] {'gx'}, use_global_device_ids=true, to_apply=%region_1.2 | all-reduce | flops 524288 | bytes 3145728 | tf_op jit(solution)/shard_map/psum | solution.py:55
  605.7 2.2 convolution_convert_fusion.1
  607.9 2.3 fusion.59
  610.3 6.4 fusion.6
  616.8 1.4 convolution_convert_fusion
  618.1 0.4 convolution_bitcast_fusion
  618.5 2.5 copy.37
  621.1 296.1 %all-reduce.12 = bf16[256,2048]{0,1:T(8,128)(2,1)S(1)} all-reduce(f32[256,2048]{0,1:T(8,128)} %bitcast.125), channel_id=1, replica_groups=mesh['gy'=4,'gx'=64] {'gx'}, use_global_device_ids=true, to_apply=%region_2.3 | all-reduce | flops 524288 | bytes 3145728 | tf_op jit(solution)/shard_map/psum | solution.py:73
  917.2 0.2 fusion.22
  917.4 0.2 fusion.20
  917.6 0.2 fusion.13
  917.8 0.2 fusion.14
  918.0 0.1 copy_bitcast_fusion
  918.1 0.7 reshape.70
  918.8 0.2 all-reduce.9.cloned.1.call-start
  919.1 7.6 fusion.7
  926.7 2.8 fusion.60
  929.4 0.0 all-gather.3.cloned.1.call-start
  929.5 0.2 fusion.23
  929.7 0.3 fusion.17
  930.0 0.2 fusion.21
  930.2 0.3 fusion.18
  930.5 0.1 pad_maximum_fusion.2
  930.6 0.7 reshape.60
  931.3 21.6 %reduce-scatter.6.cloned.1.call-done = bf16[8,2048]{1,0:T(8,128)(2,1)} async-done(((bf16[32,2048]{1,0:T(8,128)(2,1)}), bf16[8,2048]{1,0:T(8,128)(2,1)}) %reduce-scatter.6.cloned.1.call-update) | async-done | bytes 32784
  953.0 0.8 reshape.71
  953.7 0.6 convert_multiply_fusion
  954.4 247.6 %all-reduce.9.cloned.1.call-done = (f32[256,1024]{0,1:T(8,128)}, f32[1024,256]{1,0:T(8,128)}) async-done(((f32[256,1024]{0,1:T(8,128)}, f32[1024,256]{1,0:T(8,128)}), (f32[256,1024]{0,1:T(8,128)}, f32[1024,256]{1,0:T(8,128)})) %all-reduce.9.cloned.1.call-update) | async-done | bytes 2097168
  1202.0 1.3 dynamic-slice_multiply_fusion.1
  1203.2 1.3 dynamic-slice_multiply_fusion
  1204.5 6.2 reshape.59
  1210.7 6.1 copy.40
  1216.9 1.4 fusion.8
  (27 shorter events, 0.2 us)
Async XLA Ops:
  8.0 1.2 copy-start
  8.0 293.4 %copy-start.7 = (u32[256]{0:T(256)S(1)}, u32[256]{0:T(256)}, u32[]{:S(2)}) copy-start(u32[256]{0:T(256)} %constant.49) | copy-start | bytes 3076
  8.0 944.9 %reduce-scatter.6.cloned.1.call-start = ((), (), s32[]{:S(2)}) async-start(), calls=%async_computation.2 | async-start | bytes 163840
  605.7 4.6 copy-start.2
  605.7 4.6 copy-start.6
  610.2 6.5 copy-start.1
  610.3 6.5 copy-start.4
  616.8 4.3 copy-start.8
  918.8 283.1 %all-reduce.9.cloned.1.call-start = ((), (), s32[]{:S(2)}) async-start(), calls=%async_computation.3 | async-start | bytes 4194304
  919.1 7.6 copy-start.9
  926.6 2.8 copy-start.5
  929.4 287.5 %copy-start.3 = (bf16[32,64,256]{2,1,0:T(8,128)(2,1)S(1)}, bf16[32,64,256]{2,1,0:T(8,128)(2,1)}, u32[]{:S(2)}) copy-start(bf16[32,64,256]{2,1,0:T(8,128)(2,1)} %param.6) | copy-start | bytes 3145732
  929.4 275.1 %all-gather.3.cloned.1.call-start = ((), (), s32[]{:S(2)}) async-start(), calls=%async_computation.1 | async-start | bytes 1064960 | tf_op jit(solution)/shard_map/all_gather | solution.py:85
Sparse Core Ops, SparseCore 0:
  918.9 33.9 reduce-scatter.5
  954.8 102.2 all-gather.2
Sparse Core Ops, SparseCore 1:
  929.5 272.4 all-reduce.8
where the time goes:
time: 1230 us
  blocking collectives  883 us (72%)
  waiting for transfers between devices  269 us (22%)
  matrix products  31.5 us (3%)
  local copies, waits for them, and re-layouts  21.9 us (2%)
  between operations  16.4 us (1%)
    psum x1, blocking collectives, local(): lax.psum(jnp.stack([vr, vi], axis=1).reshape(chan_count, width), 'gx')  296 us
    psum x1, blocking collectives, local(): lax.psum(contract('yxo,mx->omy', piece, inverse).reshape(chan_count, widt...  296 us
    unnamed x1, blocking collectives  291 us
    unnamed x5, waiting for transfers between devices  269 us
  transfers between devices with their start and end apart: 3, of which 2 were waited for; matrix products, arithmetic and copies ran while one was open for 1% of the time, Pallas kernels for 0%

commit v1 on v0

v1 whole, which is shorter than its diff:
```python
import math

import jax
import jax.numpy as jnp
from jax import lax
from jax.sharding import PartitionSpec as P

M = 32
BF = jnp.bfloat16
F32 = jnp.float32


def bases(positions, length, modes):
    order = jnp.arange(modes, dtype=jnp.int32)
    phase = positions[:, None] * order[None, :] % length
    angle = phase.astype(F32) * (2.0 * math.pi / length)
    factor = 1.0 / math.sqrt(length)
    cosine = jnp.cos(angle) * factor
    sine = jnp.sin(angle) * factor
    weight = jnp.where(order == 0, 1.0, 2.0).astype(F32)
    forward = jnp.stack([cosine, -sine], axis=2).astype(BF)
    inverse = jnp.stack([cosine * weight, -sine * weight], axis=2).astype(BF)
    size = positions.shape[0]
    return forward.reshape(size, 2 * modes), inverse.reshape(size, 2 * modes)


def smooth_gate(values):
    return jax.nn.gelu(values, approximate=True)


def contract(form, left, right):
    return jnp.einsum(form, left, right, preferred_element_type=F32)


def local(inputs, cotangent, mode_weight, w_in, w_out):
    lines, cols, chan = inputs.shape
    nx = lax.axis_size("gx")
    ny = lax.axis_size("gy")
    chips = nx // 2
    total_x = cols * nx
    half = lines // 2
    own_rows = chan // nx
    hid = w_in.shape[1]
    me = lax.axis_index("gx")
    core = me % 2
    groups = [[2 * t + c for t in range(chips)] for c in range(2)]
    swap = [(i, i ^ 1) for i in range(nx)]

    def pair(x):
        return lax.ppermute(x, "gx", swap)

    def spread(x):
        return lax.all_to_all(x, "gx", 0, 0, tiled=True, axis_index_groups=groups)

    def pick(x, which, axis):
        return lax.dynamic_index_in_dim(x, which, axis, keepdims=False)

    inp2 = inputs.reshape(2, half, cols, chan)
    cot2 = cotangent.reshape(2, half, cols, chan)
    in_par = pair(pick(inp2, 1 - core, 0))
    cot_par = pair(pick(cot2, 1 - core, 0))
    in_own = pick(inp2, core, 0)
    cot_own = pick(cot2, core, 0)
    steps = jnp.arange(cols, dtype=jnp.int32)
    own_fwd, own_inv = bases(me * cols + steps, total_x, M)
    par_fwd, par_inv = bases((me ^ 1) * cols + steps, total_x, M)
    inv = jnp.concatenate([own_inv, par_inv], axis=0)

    spec_part = contract("yxc,xm->myc", in_own, own_fwd) + contract("yxc,xm->myc", in_par, par_fwd)
    spec_part = spec_part.astype(BF).reshape(chips, 2 * half, chan)
    weight_rows = mode_weight.transpose(1, 0, 2, 3).reshape(M, 2 * own_rows, chan)
    recv = spread(jnp.concatenate([spec_part, weight_rows], axis=1))
    spec = recv[:, : 2 * half].astype(F32).sum(0).astype(BF).reshape(2, half, chan)
    w_mine = recv[:, 2 * half :].reshape(chips, 2, own_rows, chan)
    w_par = pair(w_mine)
    w_even = jnp.where(core == 0, w_mine, w_par)
    w_odd = jnp.where(core == 0, w_par, w_mine)
    w_all = jnp.stack([w_even, w_odd], axis=1).transpose(2, 0, 1, 3, 4).reshape(2, chan, chan)
    w_re, w_im = w_all[0], w_all[1]
    u_re, u_im = spec[0], spec[1]
    vr = contract("yc,co->yo", u_re, w_re) - contract("yc,co->yo", u_im, w_im)
    vi = contract("yc,co->yo", u_re, w_im) + contract("yc,co->yo", u_im, w_re)
    mixed = jnp.concatenate([vr, vi], axis=0).astype(BF)
    mixed = spread(jnp.broadcast_to(mixed[None], (chips, 2 * half, chan)))
    mixed = mixed.reshape(2 * M, half, chan)
    spec_par = pair(spec)

    hidden = contract("myo,xm->yxo", mixed, inv).astype(BF)
    flat_g = jnp.concatenate([cot_own, cot_par], axis=1).reshape(lines * cols, chan)
    flat_h = hidden.reshape(lines * cols, chan)
    pre = jnp.dot(flat_h, w_in, preferred_element_type=F32)
    act, pullback = jax.vjp(smooth_gate, pre)
    act = act.astype(BF)
    grad_out = contract("ph,pc->hc", act, flat_g)
    grad_act = contract("pc,hc->ph", flat_g, w_out)
    d_pre = pullback(grad_act)[0].astype(BF)
    grad_in = contract("ph,pc->hc", d_pre, flat_h)
    d_hidden = contract("ph,ch->pc", d_pre, w_in).astype(BF).reshape(half, 2 * cols, chan)
    d_part = contract("yxo,xm->myo", d_hidden, inv).astype(BF).reshape(chips, 2 * half, chan)
    grads = jnp.stack([grad_in, grad_out], axis=0)
    grads = grads.reshape(2, ny, chips, 2, hid // (ny * nx), chan)
    g_par = pair(pick(grads, 1 - core, 3).astype(BF))
    g_own = pick(grads, core, 3)

    dv = spread(d_part).astype(F32).sum(0).astype(BF).reshape(2, half, chan)
    dv_par = pair(dv)
    d_re, d_im = dv[0], dv[1]
    du_re = contract("yo,co->yc", d_re, w_re) + contract("yo,co->yc", d_im, w_im)
    du_im = contract("yo,co->yc", d_im, w_re) - contract("yo,co->yc", d_re, w_im)
    du = jnp.concatenate([du_re, du_im], axis=0).astype(BF)
    u_all = jnp.concatenate([spec, spec_par], axis=1)
    d_all = jnp.concatenate([dv, dv_par], axis=1)
    g_re = contract("yc,yo->co", u_all[0], d_all[0]) + contract("yc,yo->co", u_all[1], d_all[1])
    g_im = contract("yc,yo->co", u_all[0], d_all[1]) - contract("yc,yo->co", u_all[1], d_all[0])
    mode_rows = jnp.stack([g_re, g_im], axis=0).astype(BF).reshape(2, chips, 2, own_rows, chan)
    mode_rows = pick(mode_rows, core, 2).transpose(1, 0, 2, 3).reshape(chips, 2 * own_rows, chan)
    g_sum = (g_own + g_par.astype(F32)).astype(BF)
    g_rows = g_sum.transpose(2, 0, 1, 3, 4).reshape(chips, -1, chan)
    du_rows = jnp.broadcast_to(du[None], (chips, 2 * half, chan))
    recv = spread(jnp.concatenate([du_rows, mode_rows, g_rows], axis=1))
    a, b = 2 * half, 2 * half + 2 * own_rows
    du_own = recv[:, :a]
    du_par = pair(du_own)
    mode_part = recv[:, a:b].reshape(ny, M // ny, 2 * own_rows, chan)
    g_all = recv[:, b:].astype(F32).sum(0).reshape(2, ny, hid // (ny * nx), chan)
    g_all = g_all.transpose(1, 0, 2, 3).reshape(ny, -1, chan)
    gy = lax.axis_index("gy")
    blocks = jnp.concatenate([mode_part.reshape(ny, -1, chan), g_all.astype(BF)], axis=1)
    mode_sum = pick(mode_part, gy, 0).astype(F32).reshape(-1, chan)
    total = jnp.concatenate([mode_sum, pick(g_all, gy, 0)], axis=0)
    for d in range(1, ny):
        sent = pick(blocks, (gy + d) % ny, 0)
        total = total + lax.ppermute(sent, "gy", [(i, (i + d) % ny) for i in range(ny)]).astype(F32)
    cut = mode_sum.shape[0]
    d_mode = total[:cut].reshape(M // ny, 2, own_rows, chan).transpose(1, 0, 2, 3)
    tail = total[cut:].reshape(2, hid // (ny * nx), chan)

    du_lo = jnp.where(core == 0, du_own, du_par).reshape(2 * M, half, chan)
    du_hi = jnp.where(core == 0, du_par, du_own).reshape(2 * M, half, chan)
    ret_lo = contract("myc,xm->yxc", du_lo, own_fwd)
    ret_hi = contract("myc,xm->yxc", du_hi, own_fwd)
    returned = jnp.concatenate([ret_lo, ret_hi], axis=0)
    d_inputs = (cotangent.astype(F32) + returned).astype(BF)
    scale_mlp = 1.0 / math.sqrt(lines * ny * total_x)
    scale_mode = 1.0 / math.sqrt(lines * ny)
    return (d_inputs, d_mode * scale_mode, tail[0].T * scale_mlp, tail[1] * scale_mlp)


def solution(mesh):
    placed = (P("gy", "gx", None), P("gy", "gx", None), P(None, None, "gx", None), P(), P())
    return jax.shard_map(
        local,
        mesh=mesh,
        in_specs=placed,
        out_specs=(
            P("gy", "gx", None),
            P(None, "gy", "gx", None),
            P(None, ("gy", "gx")),
            P(("gy", "gx"), None),
        ),
        check_vma=False,
    )
```

time: 1230 us -> 153 us (0.12)
  blocking collectives: 883 us -> 0 us
  waiting for transfers between devices: 269 us -> 40.3 us
  starting transfers between devices: 0.3 us -> 40.1 us
  between operations: 16.4 us -> 1.26 us
    psum x2 -> x0, blocking collectives: 592 us -> none  [the longest x1 296 us: local(): lax.psum(jnp.stack([vr, vi], axis=1).reshape(chan_count, width), 'gx')]
    unnamed x1 -> x0, blocking collectives: 291 us -> none
    unnamed x5 -> x0, waiting for transfers between devices: 269 us -> none
    all_to_all x0 -> x4, waiting for transfers between devices: none -> 34.8 us  [spread(): return lax.all_to_all(x, 'gx', 0, 0, tiled=True, axis_index_groups=groups)]
    all_to_all x0 -> x4, starting transfers between devices: none -> 28.7 us  [spread(): return lax.all_to_all(x, 'gx', 0, 0, tiled=True, axis_index_groups=groups)]
    another operation x1 -> x10, local copies, waits for them, and re-layouts: 0.01 us -> 14.6 us  [local(): jnp.stack([du_re, du_im], axis=1).astype(jnp.bfloat16)]
    dot_general x21 -> x23, matrix products: 31.5 us -> 38.2 us  [the longest x22 26.8 us: contract(): return jnp.einsum(form, left, right, preferred_element_type=F32)]
  transfers between devices with their start and end apart: 3 -> 14, of which waited for: 2 -> 8; matrix products, arithmetic and copies ran while one was open for 1% -> 26% of each run, Pallas kernels for 0% -> 0%
where the time goes in v1:
time: 153 us; the launch traced here: 151 us
  waiting for transfers between devices  40.3 us (26%)
  starting transfers between devices  40.1 us (26%)
  matrix products  38.2 us (25%)
  local copies, waits for them, and re-layouts  22.4 us (15%)
  other arithmetic  8.51 us (6%)
    all_to_all x4, waiting for transfers between devices, spread(): return lax.all_to_all(x, 'gx', 0, 0, tiled=True, axis_index_groups=groups)  34.8 us
    all_to_all x4, starting transfers between devices, spread(): return lax.all_to_all(x, 'gx', 0, 0, tiled=True, axis_index_groups=groups)  28.7 us
    dot_general x22, matrix products, contract(): return jnp.einsum(form, left, right, preferred_element_type=F32)  26.8 us
    another operation x2, local copies, waits for them, and re-layouts  14.4 us
    dot_general x1, matrix products, local(): pre = jnp.dot(flat_h, w_in, preferred_element_type=F32)  11.4 us
    ppermute x3, starting transfers between devices, local(): lax.ppermute(sent, 'gy', [(i, (i + d) % ny) for i in range(ny)]).astype(F32)  10.5 us
    ppermute x7, waiting for transfers between devices, pair(): return lax.ppermute(x, 'gx', swap)  4.15 us
  transfers between devices with their start and end apart: 14, of which 8 were waited for; matrix products, arithmetic and copies ran while one was open for 26% of the time, Pallas kernels for 0%

profile of v1, /device:TPU:2, one launch (start us, length us, event | category | flops | bytes accessed | tf_op | source)
XLA Modules:
  0.0 150.9 jit_solution(4563732597803720856)
XLA Ops:
  0.7 1.2 copy-done
  2.3 0.9 copy.84
  3.3 0.3 fusion.48
  3.6 0.5 collective-permute-done.1
  4.0 1.3 fusion.34
  5.3 0.3 copy.83
  5.7 0.9 pad_maximum_fusion.2
  6.5 9.0 %all-to-all-start = ((bf16[32,40,256]{2,1,0:T(8,128)(2,1)}), bf16[32,40,256]{2,1,0:T(8,128)(2,1)S(1)}, u32[]{:S(2)}, u32[]{:S(2)}) async-start(bf16[32,40,256]{2,1,0:T(8,128)(2,1)} %pad_maximum_fusion.2), calls=%async_computation | async-start | bytes 1310720 | tf_op jit(solution)/shard_map/all_to_all | solution.py:53
  15.5 1.1 dynamic-slice_bitcast_fusion.2
  16.6 11.6 %all-to-all-done = bf16[32,40,256]{2,1,0:T(8,128)(2,1)S(1)} async-done(((bf16[32,40,256]{2,1,0:T(8,128)(2,1)}), bf16[32,40,256]{2,1,0:T(8,128)(2,1)S(1)}, u32[]{:S(2)}, u32[]{:S(2)}) %all-to-all-start) | async-done | bytes 655392 | tf_op jit(solution)/shard_map/all_to_all | solution.py:53
  28.5 1.3 collective-permute-done.2
  30.8 0.9 broadcast_in_dim.16
  31.7 5.7 %all-to-all-start.1 = ((bf16[32,32,256]{2,1,0:T(8,128)(2,1)}), bf16[32,32,256]{2,1,0:T(8,128)(2,1)}, u32[]{:S(2)}, u32[]{:S(2)}) async-start(bf16[32,32,256]{2,1,0:T(8,128)(2,1)} %broadcast_in_dim.16), calls=%async_computation.1 | async-start | bytes 1048576 | tf_op jit(solution)/shard_map/all_to_all | solution.py:53
  37.5 1.3 pad_maximum_fusion.1
  38.7 5.6 %fusion.121 = f32[2048,1024]{0,1:T(8,128)} fusion(bf16[2048,256]{1,0:T(8,128)(2,1)S(1)} %bitcast.169, bf16[1024,256]{1,0:T(8,128)(2,1)} %param.9), kind=kOutput, calls=%fused_computation.190 | convolution fusion | flops 1073741824 | bytes 9961472 | tf_op jit(solution)/shard_map/pc,hc->ph/dot_general | solution.py:32
  44.4 4.8 %all-to-all-done.1 = bf16[32,32,256]{2,1,0:T(8,128)(2,1)} async-done(((bf16[32,32,256]{2,1,0:T(8,128)(2,1)}), bf16[32,32,256]{2,1,0:T(8,128)(2,1)}, u32[]{:S(2)}, u32[]{:S(2)}) %all-to-all-start.1) | async-done | bytes 524320 | tf_op jit(solution)/shard_map/all_to_all | solution.py:53
  49.1 1.7 %convolution_convert_fusion = bf16[128,16,256]{2,0,1:T(8,128)(2,1)S(1)} fusion(bf16[64,16,256]{2,1,0:T(8,128)(2,1)} %bitcast.22, bf16[64,64]{0,1:T(8,128)(2,1)S(1)} %bitcast.200, bf16[64,64]{0,1:T(8,128)(2,1)S(1)} %bitcast.198), kind=kOutput, calls=%fused_computation.37 | convolution fusion | flops 67665920 | bytes 1589248 | tf_op jit(solution)/shard_map/myo,xm->yxo/dot_general | solution.py:32
  50.9 11.4 %fusion.14 = (bf16[1024,2048]{1,0:T(8,128)(2,1)}, bf16[1024,2048]{1,0:T(8,128)(2,1)}, f32[2048,1024]{0,1:T(8,128)S(1)}) fusion(f32[2048,1024]{0,1:T(8,128)} %fusion.121, bf16[2048,256]{1,0:T(8,128)(2,1)S(1)} %bitcast.177, bf16[256,1024]{1,0:T(8,128)(2,1)} %param.8), kind=kOutput, calls=%fused_computation.20 | convolution fusion | flops 1119879168 | bytes 26738688 | tf_op jit(solution)/shard_map/dot_general | solution.py:91
  62.3 6.8 %fusion.24 = bf16[2048,256]{1,0:T(8,128)(2,1)S(1)} fusion(bf16[256,1024]{1,0:T(8,128)(2,1)S(1)} %copy-done.5, f32[2048,1024]{0,1:T(8,128)S(1)} %get-tuple-element.27, f32[2048,1024]{0,1:T(8,128)S(1)} %bitcast.168), kind=kOutput, calls=%fused_computation.30 | convolution fusion | flops 1116209152 | bytes 18350080 | tf_op jit(solution)/shard_map/ph,ch->pc/dot_general | solution.py:32
  69.1 0.3 convolution_convert_fusion.1
  69.5 1.1 copy.91
  70.6 5.7 %all-to-all-start.2 = ((bf16[32,32,256]{2,1,0:T(8,128)(2,1)}), bf16[32,32,256]{2,1,0:T(8,128)(2,1)}, u32[]{:S(2)}, u32[]{:S(2)}) async-start(bf16[32,32,256]{2,1,0:T(8,128)(2,1)} %bitcast.174), calls=%async_computation.2 | async-start | bytes 1048576 | tf_op jit(solution)/shard_map/all_to_all | solution.py:53
  76.2 7.2 %reshape.592 = bf16[4,32,2,4,2048]{4,3,2,1,0:T(4,128)(2,1)} reshape(bf16[1024,2048]{1,0:T(8,128)(2,1)} %get-tuple-element.4) | data formatting | bytes 8388608 | tf_op jit(solution)/shard_map/reshape.310
  83.4 7.2 %reshape.591 = bf16[4,32,2,4,2048]{4,3,2,1,0:T(4,128)(2,1)} reshape(bf16[1024,2048]{1,0:T(8,128)(2,1)} %get-tuple-element.5) | data formatting | bytes 8388608 | tf_op jit(solution)/shard_map/reshape.308
  90.7 5.2 %fusion.31 = f32[1,4,32,2,4,256]{5,2,4,3,1,0:T(8,128)S(1)} fusion(bf16[2048,256,1,1,1]{1,0,4,3,2:T(8,128)(2,1)S(1)} %bitcast.170, bf16[4,32,2,4,2048]{4,3,2,1,0:T(4,128)(2,1)} %reshape.592), kind=kOutput, calls=%fused_computation.41 | convolution fusion | flops 1073741824 | bytes 6291456 | tf_op jit(solution)/shard_map/ph,pc->hc/dot_general | solution.py:32
  95.9 2.8 %fusion.28 = f32[1,4,32,2,4,256]{5,2,4,3,1,0:T(8,128)S(1)} fusion(bf16[2048,256,1,1,1]{1,0,4,3,2:T(8,128)(2,1)S(1)} %bitcast.178, bf16[4,32,2,4,2048]{4,3,2,1,0:T(4,128)(2,1)S(1)} %copy-done.1), kind=kOutput, calls=%fused_computation.40 | convolution fusion | flops 1073741824 | bytes 6291456 | tf_op jit(solution)/shard_map/ph,pc->hc/dot_general | solution.py:32
  98.9 0.5 collective-permute-start.3
  99.4 1.4 collective-permute-done.5
  101.0 0.3 copy.97
  101.3 1.1 reduce_sum.34
  103.3 1.0 collective-permute-done.4
  104.6 0.2 fusion.36
  104.9 0.2 fusion.101
  105.1 0.2 fusion.35
  105.5 1.1 pad_maximum_fusion
  106.6 8.4 %all-to-all-start.3 = ((bf16[32,72,256]{2,1,0:T(8,128)(2,1)}), bf16[32,72,256]{2,1,0:T(8,128)(2,1)S(1)}, u32[]{:S(2)}, u32[]{:S(2)}) async-start(bf16[32,72,256]{2,1,0:T(8,128)(2,1)} %pad_maximum_fusion), calls=%async_computation.3 | async-start | bytes 2359296 | tf_op jit(solution)/shard_map/all_to_all | solution.py:53
  115.1 18.4 %all-to-all-done.3 = bf16[32,72,256]{2,1,0:T(8,128)(2,1)S(1)} async-done(((bf16[32,72,256]{2,1,0:T(8,128)(2,1)}), bf16[32,72,256]{2,1,0:T(8,128)(2,1)S(1)}, u32[]{:S(2)}, u32[]{:S(2)}) %all-to-all-start.3) | async-done | bytes 1179680 | tf_op jit(solution)/shard_map/all_to_all | solution.py:53
  133.7 3.3 %collective-permute-start.7 = (bf16[72,256]{1,0:T(8,128)(2,1)S(1)}, bf16[72,256]{1,0:T(8,128)(2,1)S(1)}, u32[]{:S(2)}, u32[]{:S(2)}) collective-permute-start(bf16[72,256]{1,0:T(8,128)(2,1)S(1)} %get-tuple-element.14), channel_id=1, source_target_pairs={{0,64},{64,128},{128,192},{192,0},{1,65},{65,129},{129,193},{193,1... | collective-permute-start | bytes 110600 | tf_op jit(solution)/shard_map/ppermute | solution.py:133
  137.0 4.5 %collective-permute-start.8 = (bf16[72,256]{1,0:T(8,128)(2,1)S(1)}, bf16[72,256]{1,0:T(8,128)(2,1)S(1)}, u32[]{:S(2)}, u32[]{:S(2)}) collective-permute-start(bf16[72,256]{1,0:T(8,128)(2,1)S(1)} %get-tuple-element.15), channel_id=1, source_target_pairs={{0,128},{64,192},{128,0},{192,64},{1,129},{65,193},{129,1},{193,65... | collective-permute-start | bytes 110600 | tf_op jit(solution)/shard_map/ppermute | solution.py:133
  141.5 2.7 %collective-permute-start.9 = (bf16[72,256]{1,0:T(8,128)(2,1)S(1)}, bf16[72,256]{1,0:T(8,128)(2,1)S(1)}, u32[]{:S(2)}, u32[]{:S(2)}) collective-permute-start(bf16[72,256]{1,0:T(8,128)(2,1)S(1)} %get-tuple-element.16), channel_id=1, source_target_pairs={{0,192},{64,0},{128,64},{192,128},{1,193},{65,1},{129,65},{193,129... | collective-permute-start | bytes 110600 | tf_op jit(solution)/shard_map/ppermute | solution.py:133
  144.2 0.9 slice.99
  145.1 1.4 collective-permute-done.9
  146.5 0.6 copy.130
  147.1 0.6 slice_multiply_fusion.1
  147.8 1.1 broadcast_select_fusion.1
  148.9 0.3 convolution_bitcast_fusion.1
  149.2 0.3 convolution_bitcast_fusion
  149.5 1.4 fusion.27
  (83 shorter events, 3.8 us)
Async XLA Ops:
  0.6 1.2 copy-start
  0.6 14.9 %copy-start.2 = (bf16[32,64,256]{2,1,0:T(8,128)(2,1)S(1)}, bf16[32,64,256]{2,1,0:T(8,128)(2,1)}, u32[]{:S(2)}) copy-start(bf16[32,64,256]{2,1,0:T(8,128)(2,1)} %param.6) | copy-start | bytes 3145732
  1.9 2.1 %collective-permute-start.1 = (bf16[16,64,256]{2,1,0:T(8,128)(2,1)S(1)}, bf16[16,64,256]{2,1,0:T(8,128)(2,1)}, u32[]{:S(2)}, u32[]{:S(2)}) collective-permute-start(bf16[16,64,256]{2,1,0:T(8,128)(2,1)S(1)} %dynamic-slice_bitcast_fusion), channel_id=1, source_target_pairs={{0,1},{1,0},{2,3},{3,2},{4,5},{5,4},{6,7},{7,6},{8,9},{9,8},{10,11... | collective-permute-start | bytes 1572872 | tf_op jit(solution)/shard_map/ppermute | solution.py:50
  6.5 21.7 %all-to-all-start = ((bf16[32,40,256]{2,1,0:T(8,128)(2,1)}), bf16[32,40,256]{2,1,0:T(8,128)(2,1)S(1)}, u32[]{:S(2)}, u32[]{:S(2)}) async-start(bf16[32,40,256]{2,1,0:T(8,128)(2,1)} %pad_maximum_fusion.2), calls=%async_computation | async-start | bytes 1310720 | tf_op jit(solution)/shard_map/all_to_all | solution.py:53
  16.6 20.9 %collective-permute-start = (bf16[16,64,256]{2,1,0:T(8,128)(2,1)}, bf16[16,64,256]{2,1,0:T(8,128)(2,1)}, u32[]{:S(2)}, u32[]{:S(2)}) collective-permute-start(bf16[16,64,256]{2,1,0:T(8,128)(2,1)} %get-tuple-element.9), channel_id=1, source_target_pairs={{0,1},{1,0},{2,3},{3,2},{4,5},{5,4},{6,7},{7,6},{8,9},{9,8},{10,11... | collective-permute-start | bytes 1572872 | tf_op jit(solution)/shard_map/ppermute | solution.py:50
  28.3 1.4 collective-permute-start.2
  31.7 17.4 %all-to-all-start.1 = ((bf16[32,32,256]{2,1,0:T(8,128)(2,1)}), bf16[32,32,256]{2,1,0:T(8,128)(2,1)}, u32[]{:S(2)}, u32[]{:S(2)}) async-start(bf16[32,32,256]{2,1,0:T(8,128)(2,1)} %broadcast_in_dim.16), calls=%async_computation.1 | async-start | bytes 1048576 | tf_op jit(solution)/shard_map/all_to_all | solution.py:53
  49.1 13.2 %slice-start = ((s8[8388608]{0:T(1024)(128)(4,1)}), s8[4194304]{0:T(1024)(128)(4,1)S(1)}, s32[]{:S(2)}) async-start(s8[8388608]{0:T(1024)(128)(4,1)} %bitcast.167), calls=%async_computation.4 | async-start | bytes 8388608
  50.8 11.4 %copy-start.3 = (bf16[128,16,256]{2,0,1:T(8,128)(2,1)}, bf16[128,16,256]{2,0,1:T(8,128)(2,1)S(1)}, u32[]{:S(2)}) copy-start(bf16[128,16,256]{2,0,1:T(8,128)(2,1)S(1)} %convolution_convert_fusion) | copy-start | bytes 3145732
  50.9 11.4 %slice-start.1 = ((s8[8388608]{0:T(1024)(128)(4,1)}), s8[4194304]{0:T(1024)(128)(4,1)S(1)}, s32[]{:S(2)}) async-start(s8[8388608]{0:T(1024)(128)(4,1)} %bitcast.167), calls=%async_computation.5 | async-start | bytes 8388608
  50.9 11.4 %copy-start.5 = (bf16[256,1024]{1,0:T(8,128)(2,1)S(1)}, bf16[256,1024]{1,0:T(8,128)(2,1)}, u32[]{:S(2)}) copy-start(bf16[256,1024]{1,0:T(8,128)(2,1)} %param.8) | copy-start | bytes 1572868
  70.6 30.7 %all-to-all-start.2 = ((bf16[32,32,256]{2,1,0:T(8,128)(2,1)}), bf16[32,32,256]{2,1,0:T(8,128)(2,1)}, u32[]{:S(2)}, u32[]{:S(2)}) async-start(bf16[32,32,256]{2,1,0:T(8,128)(2,1)} %bitcast.174), calls=%async_computation.2 | async-start | bytes 1048576 | tf_op jit(solution)/shard_map/all_to_all | solution.py:53
  90.7 5.2 %copy-start.1 = (bf16[4,32,2,4,2048]{4,3,2,1,0:T(4,128)(2,1)S(1)}, bf16[4,32,2,4,2048]{4,3,2,1,0:T(4,128)(2,1)}, u32[]{:S(2)}) copy-start(bf16[4,32,2,4,2048]{4,3,2,1,0:T(4,128)(2,1)} %reshape.591) | copy-start | bytes 12582916
  90.7 5.2 %copy-start.4 = (bf16[128,16,256]{2,0,1:T(8,128)(2,1)S(1)}, bf16[128,16,256]{2,0,1:T(8,128)(2,1)}, u32[]{:S(2)}) copy-start(bf16[128,16,256]{2,0,1:T(8,128)(2,1)} %copy-done.3) | copy-start | bytes 3145732
  98.8 2.0 %collective-permute-start.5 = (bf16[2,4,32,4,256]{4,2,3,1,0:T(8,128)(2,1)S(1)}, bf16[2,4,32,4,256]{4,2,3,1,0:T(8,128)(2,1)S(1)}, u32[]{:S(2)}, u32[]{:S(2)}) collective-permute-start(bf16[2,4,32,4,256]{4,2,3,1,0:T(8,128)(2,1)S(1)} %fusion.47), channel_id=1, source_target_pairs={{0,1},{1,0},{2,3},{3,2},{4,5},{5,4},{6,7},{7,6},{8,9},{9,8},{10,11... | collective-permute-start | bytes 1572872 | tf_op jit(solution)/shard_map/ppermute | solution.py:50
  98.9 4.4 %collective-permute-start.3 = (bf16[2,16,256]{2,1,0:T(8,128)(2,1)S(1)}, bf16[2,16,256]{2,1,0:T(8,128)(2,1)S(1)}, u32[]{:S(2)}, u32[]{:S(2)}) collective-permute-start(bf16[2,16,256]{2,1,0:T(8,128)(2,1)S(1)} %bitcast.180), channel_id=1, source_target_pairs={{0,1},{1,0},{2,3},{3,2},{4,5},{5,4},{6,7},{7,6},{8,9},{9,8},{10,11... | collective-permute-start | bytes 49160 | tf_op jit(solution)/shard_map/ppermute | solution.py:50
  103.1 1.2 collective-permute-start.4
  106.6 26.8 %all-to-all-start.3 = ((bf16[32,72,256]{2,1,0:T(8,128)(2,1)}), bf16[32,72,256]{2,1,0:T(8,128)(2,1)S(1)}, u32[]{:S(2)}, u32[]{:S(2)}) async-start(bf16[32,72,256]{2,1,0:T(8,128)(2,1)} %pad_maximum_fusion), calls=%async_computation.3 | async-start | bytes 2359296 | tf_op jit(solution)/shard_map/all_to_all | solution.py:53
  133.7 11.4 %collective-permute-start.7 = (bf16[72,256]{1,0:T(8,128)(2,1)S(1)}, bf16[72,256]{1,0:T(8,128)(2,1)S(1)}, u32[]{:S(2)}, u32[]{:S(2)}) collective-permute-start(bf16[72,256]{1,0:T(8,128)(2,1)S(1)} %get-tuple-element.14), channel_id=1, source_target_pairs={{0,64},{64,128},{128,192},{192,0},{1,65},{65,129},{129,193},{193,1... | collective-permute-start | bytes 110600 | tf_op jit(solution)/shard_map/ppermute | solution.py:133
  137.0 8.1 %collective-permute-start.8 = (bf16[72,256]{1,0:T(8,128)(2,1)S(1)}, bf16[72,256]{1,0:T(8,128)(2,1)S(1)}, u32[]{:S(2)}, u32[]{:S(2)}) collective-permute-start(bf16[72,256]{1,0:T(8,128)(2,1)S(1)} %get-tuple-element.15), channel_id=1, source_target_pairs={{0,128},{64,192},{128,0},{192,64},{1,129},{65,193},{129,1},{193,65... | collective-permute-start | bytes 110600 | tf_op jit(solution)/shard_map/ppermute | solution.py:133
  141.5 5.0 %collective-permute-start.9 = (bf16[72,256]{1,0:T(8,128)(2,1)S(1)}, bf16[72,256]{1,0:T(8,128)(2,1)S(1)}, u32[]{:S(2)}, u32[]{:S(2)}) collective-permute-start(bf16[72,256]{1,0:T(8,128)(2,1)S(1)} %get-tuple-element.16), channel_id=1, source_target_pairs={{0,192},{64,0},{128,64},{192,128},{1,193},{65,1},{129,65},{193,129... | collective-permute-start | bytes 110600 | tf_op jit(solution)/shard_map/ppermute | solution.py:133
  145.0 2.7 %collective-permute-start.6 = (bf16[32,32,256]{2,1,0:T(8,128)(2,1)}, bf16[32,32,256]{2,1,0:T(8,128)(2,1)}, u32[]{:S(2)}, u32[]{:S(2)}) collective-permute-start(bf16[32,32,256]{2,1,0:T(8,128)(2,1)} %slice.99), channel_id=1, source_target_pairs={{0,1},{1,0},{2,3},{3,2},{4,5},{5,4},{6,7},{7,6},{8,9},{9,8},{10,11... | collective-permute-start | bytes 1572872 | tf_op jit(solution)/shard_map/ppermute | solution.py:50

commit v2 on v1

v2 whole, which is shorter than its diff:
```python
import math

import jax
import jax.numpy as jnp
from jax import lax
from jax.experimental import pallas as pl
from jax.experimental.pallas import tpu as pltpu
from jax.sharding import PartitionSpec as P

M = 32
LANES = 128
BF = jnp.bfloat16
F32 = jnp.float32


def bases(positions, length, modes):
    order = jnp.arange(modes, dtype=jnp.int32)
    phase = positions[:, None] * order[None, :] % length
    angle = phase.astype(F32) * (2.0 * math.pi / length)
    factor = 1.0 / math.sqrt(length)
    cosine = jnp.cos(angle) * factor
    sine = jnp.sin(angle) * factor
    weight = jnp.where(order == 0, 1.0, 2.0).astype(F32)
    forward = jnp.stack([cosine, -sine], axis=2).astype(BF)
    inverse = jnp.stack([cosine * weight, -sine * weight], axis=2).astype(BF)
    size = positions.shape[0]
    return forward.reshape(size, 2 * modes), inverse.reshape(size, 2 * modes)


def contract(form, left, right):
    return jnp.einsum(form, left, right, preferred_element_type=F32)


def dot(left, right):
    return jnp.dot(left, right, preferred_element_type=F32)


def rows_dot(left, right):
    return lax.dot_general(left, right, (((0,), (0,)), ((), ())), preferred_element_type=F32)


def grad_act_kernel(own_ref, par_ref, wt_ref, out_ref):
    block, cols, _ = own_ref.shape
    for y in range(block):
        base = 2 * cols * y
        out_ref[base : base + cols, :] = dot(own_ref[y], wt_ref[...])
        out_ref[base + cols : base + 2 * cols, :] = dot(par_ref[y], wt_ref[...])


def grad_act_call(own, par, w_out_t):
    half, cols, chan = own.shape
    hid = w_out_t.shape[1]
    block = 4
    return pl.pallas_call(
        grad_act_kernel,
        grid=(half // block,),
        in_specs=[
            pl.BlockSpec((block, cols, chan), lambda i: (i, 0, 0)),
            pl.BlockSpec((block, cols, chan), lambda i: (i, 0, 0)),
            pl.BlockSpec((chan, hid), lambda i: (0, 0)),
        ],
        out_specs=pl.BlockSpec((block * 2 * cols, hid), lambda i: (i, 0)),
        out_shape=jax.ShapeDtypeStruct((half * 2 * cols, hid), F32),
        name="grad_act",
    )(own, par, w_out_t)


GELU_A = math.sqrt(2.0 / math.pi)
GELU_B = 0.044715 * GELU_A


def mlp_kernel(mix_ref, ga_ref, inv_ref, invt_ref, wi_ref, wit_ref, hid_ref, act_ref, dpre_ref, part_ref, mix_lo, mix_hi, part_lo, part_hi):
    i = pl.program_id(0)
    rows, _ = hid_ref.shape
    cols = inv_ref.shape[0]
    block = rows // cols
    modes = inv_ref.shape[1]
    half = mix_ref.shape[0] // modes
    width = wi_ref.shape[1]
    piece = 256

    @pl.when(i == 0)
    def _():
        mix_lo[...] = mix_ref[:, :LANES].astype(F32)
        mix_hi[...] = mix_ref[:, LANES:].astype(F32)

    for b in range(block):
        lines = pl.ds(i * block + b, modes, stride=half)
        table = jnp.concatenate([mix_lo[lines, :], mix_hi[lines, :]], axis=1).astype(BF)
        hid_ref[b * cols : (b + 1) * cols, :] = dot(inv_ref[...], table).astype(BF)
    hidden = hid_ref[...]
    total = None
    for start in range(0, width, piece):
        sl = slice(start, start + piece)
        p = dot(hidden, wi_ref[:, sl])
        sq = p * p
        t = jnp.tanh(p * (GELU_A + GELU_B * sq))
        s = 0.5 + 0.5 * t
        act = p * s
        slope = s + act * (1.0 - s) * (2.0 * GELU_A + (6.0 * GELU_B) * sq)
        act_ref[:, sl] = act.astype(BF)
        d_pre = (ga_ref[:, sl] * slope).astype(BF)
        dpre_ref[:, sl] = d_pre
        term = dot(d_pre, wit_ref[sl, :])
        total = term if total is None else total + term
    d_hidden = total.astype(BF)
    for b in range(block):
        lines = pl.ds(i * block + b, modes, stride=half)
        sums = dot(invt_ref[...], d_hidden[b * cols : (b + 1) * cols])
        part_lo[lines, :] = sums[:, :LANES]
        part_hi[lines, :] = sums[:, LANES:]

    @pl.when(i == pl.num_programs(0) - 1)
    def _():
        part_ref[:, :LANES] = part_lo[...].astype(BF)
        part_ref[:, LANES:] = part_hi[...].astype(BF)


def mlp_call(mix, ga, inv, w_in, block=2):
    cols, modes = inv.shape
    chan, width = w_in.shape
    half = mix.shape[0] // modes
    rows = block * cols
    whole = lambda i: (0, 0)
    step = lambda i: (i, 0)
    return pl.pallas_call(
        mlp_kernel,
        grid=(half // block,),
        in_specs=[
            pl.BlockSpec((modes * half, chan), whole),
            pl.BlockSpec((rows, width), step),
            pl.BlockSpec((cols, modes), whole),
            pl.BlockSpec((modes, cols), whole),
            pl.BlockSpec((chan, width), whole),
            pl.BlockSpec((width, chan), whole),
        ],
        out_specs=[
            pl.BlockSpec((rows, chan), step),
            pl.BlockSpec((rows, width), step),
            pl.BlockSpec((rows, width), step),
            pl.BlockSpec((modes * half, chan), whole),
        ],
        out_shape=[
            jax.ShapeDtypeStruct((half * cols, chan), BF),
            jax.ShapeDtypeStruct((half * cols, width), BF),
            jax.ShapeDtypeStruct((half * cols, width), BF),
            jax.ShapeDtypeStruct((modes * half, chan), BF),
        ],
        scratch_shapes=[pltpu.VMEM((modes * half, LANES), F32)] * 4,
        name="mlp",
    )(mix, ga, inv, inv.T, w_in, w_in.T)


def grads_kernel(core_ref, hid_ref, dpre_ref, act_ref, own_ref, par_ref, keep_ref, send_ref, acc_in, acc_out):
    i = pl.program_id(0)
    block, _, _ = own_ref.shape
    chips, kept, _ = keep_ref.shape
    groups = kept // 8

    @pl.when(i == 0)
    def _():
        acc_in[...] = jnp.zeros_like(acc_in)
        acc_out[...] = jnp.zeros_like(acc_out)

    acc_in[...] += rows_dot(hid_ref[...], dpre_ref[...])
    cot = jnp.concatenate([r[b] for b in range(block) for r in (own_ref, par_ref)], axis=0)
    acc_out[...] += rows_dot(cot, act_ref[...])

    def store(ref, acc):
        full = acc[...].T
        for t in range(chips):
            for g in range(groups):
                top = (g * chips + t) * 8
                if ref.dtype == F32:
                    ref[t, g * 8 : (g + 1) * 8, :] = full[top : top + 8]
            if ref.dtype != F32:
                ref[t] = jnp.concatenate(
                    [full[(g * chips + t) * 8 : (g * chips + t) * 8 + 8] for g in range(groups)], axis=0
                ).astype(ref.dtype)

    last = i == pl.num_programs(0) - 1

    @pl.when(last & (core_ref[0] == 0))
    def _():
        store(keep_ref, acc_in)
        store(send_ref, acc_out)

    @pl.when(last & (core_ref[0] != 0))
    def _():
        store(keep_ref, acc_out)
        store(send_ref, acc_in)


def grads_call(core, hidden, d_pre, act, own, par, chips, block=4):
    half, cols, chan = own.shape
    width = act.shape[1]
    rows = block * 2 * cols
    kept = width // chips
    step = lambda i, c: (i, 0)
    line = lambda i, c: (i, 0, 0)
    whole = lambda i, c: (0, 0, 0)
    return pl.pallas_call(
        grads_kernel,
        grid_spec=pltpu.PrefetchScalarGridSpec(
            num_scalar_prefetch=1,
            grid=(half // block,),
            in_specs=[
                pl.BlockSpec((rows, chan), step),
                pl.BlockSpec((rows, width), step),
                pl.BlockSpec((rows, width), step),
                pl.BlockSpec((block, cols, chan), line),
                pl.BlockSpec((block, cols, chan), line),
            ],
            out_specs=[
                pl.BlockSpec((chips, kept, chan), whole),
                pl.BlockSpec((chips, kept, chan), whole),
            ],
            scratch_shapes=[pltpu.VMEM((chan, width), F32), pltpu.VMEM((chan, width), F32)],
        ),
        out_shape=[
            jax.ShapeDtypeStruct((chips, kept, chan), F32),
            jax.ShapeDtypeStruct((chips, kept, chan), BF),
        ],
        name="grads",
    )(core.reshape(1), hidden, d_pre, act, own, par)


def local(inputs, cotangent, mode_weight, w_in, w_out):
    lines, cols, chan = inputs.shape
    nx = lax.axis_size("gx")
    ny = lax.axis_size("gy")
    chips = nx // 2
    total_x = cols * nx
    half = lines // 2
    own_rows = chan // nx
    me = lax.axis_index("gx")
    core = me % 2
    groups = [[2 * t + c for t in range(chips)] for c in range(2)]
    swap = [(i, i ^ 1) for i in range(nx)]

    def pair(x):
        return lax.ppermute(x, "gx", swap)

    def spread(x):
        return lax.all_to_all(x, "gx", 0, 0, tiled=True, axis_index_groups=groups)

    def pick(x, which, axis):
        return lax.dynamic_index_in_dim(x, which, axis, keepdims=False)

    inp2 = inputs.reshape(2, half, cols, chan)
    cot2 = cotangent.reshape(2, half, cols, chan)
    in_par = pair(pick(inp2, 1 - core, 0))
    cot_par = pair(pick(cot2, 1 - core, 0))
    in_own = pick(inp2, core, 0)
    cot_own = pick(cot2, core, 0)
    steps = jnp.arange(cols, dtype=jnp.int32)
    own_fwd, own_inv = bases(me * cols + steps, total_x, M)
    par_fwd, par_inv = bases((me ^ 1) * cols + steps, total_x, M)
    inv = jnp.concatenate([own_inv, par_inv], axis=0)

    spec_part = contract("yxc,xm->myc", in_own, own_fwd) + contract("yxc,xm->myc", in_par, par_fwd)
    spec_part = spec_part.astype(BF).reshape(chips, 2 * half, chan)
    weight_rows = mode_weight.transpose(1, 0, 2, 3).reshape(M, 2 * own_rows, chan)
    recv = spread(jnp.concatenate([spec_part, weight_rows], axis=1))
    grad_act = grad_act_call(cot_own, cot_par, w_out.T)
    spec = recv[:, : 2 * half].astype(F32).sum(0).astype(BF).reshape(2, half, chan)
    w_mine = recv[:, 2 * half :].reshape(chips, 2, own_rows, chan)
    w_par = pair(w_mine)
    w_even = jnp.where(core == 0, w_mine, w_par)
    w_odd = jnp.where(core == 0, w_par, w_mine)
    w_all = jnp.stack([w_even, w_odd], axis=1).transpose(2, 0, 1, 3, 4).reshape(2, chan, chan)
    w_re, w_im = w_all[0], w_all[1]
    u_re, u_im = spec[0], spec[1]
    vr = contract("yc,co->yo", u_re, w_re) - contract("yc,co->yo", u_im, w_im)
    vi = contract("yc,co->yo", u_re, w_im) + contract("yc,co->yo", u_im, w_re)
    mixed = jnp.concatenate([vr, vi], axis=0).astype(BF)
    mixed = spread(jnp.broadcast_to(mixed[None], (chips, 2 * half, chan)))
    spec_par = pair(spec)

    hidden, act, d_pre, d_part = mlp_call(mixed.reshape(2 * M * half, chan), grad_act, inv, w_in)
    dv = spread(d_part.reshape(chips, 2 * half, chan))
    g_own, g_send = grads_call(core, hidden, d_pre, act, cot_own, cot_par, chips)
    g_par = pair(g_send)
    dv = dv.astype(F32).sum(0).astype(BF).reshape(2, half, chan)
    dv_par = pair(dv)
    d_re, d_im = dv[0], dv[1]
    du_re = contract("yo,co->yc", d_re, w_re) + contract("yo,co->yc", d_im, w_im)
    du_im = contract("yo,co->yc", d_im, w_re) - contract("yo,co->yc", d_re, w_im)
    du = jnp.concatenate([du_re, du_im], axis=0).astype(BF)
    u_all = jnp.concatenate([spec, spec_par], axis=1)
    d_all = jnp.concatenate([dv, dv_par], axis=1)
    g_re = contract("yc,yo->co", u_all[0], d_all[0]) + contract("yc,yo->co", u_all[1], d_all[1])
    g_im = contract("yc,yo->co", u_all[0], d_all[1]) - contract("yc,yo->co", u_all[1], d_all[0])
    mode_rows = jnp.stack([g_re, g_im], axis=0).astype(BF).reshape(2, chips, 2, own_rows, chan)
    mode_rows = pick(mode_rows, core, 2).transpose(1, 0, 2, 3).reshape(chips, 2 * own_rows, chan)
    g_rows = (g_own + g_par.astype(F32)).astype(BF)
    du_rows = jnp.broadcast_to(du[None], (chips, 2 * half, chan))
    recv = spread(jnp.concatenate([du_rows, g_rows, mode_rows], axis=1))
    du_own = recv[:, : 2 * half]
    recv = recv[:, 2 * half :]
    du_par = pair(du_own)
    cut = g_rows.shape[1]
    g_all = recv[:, :cut].astype(F32).sum(0).astype(BF).reshape(ny, 2 * own_rows, chan)
    mode_part = recv[:, cut:].reshape(ny, (M // ny) * 2 * own_rows, chan)
    blocks = jnp.concatenate([g_all, mode_part], axis=1)
    total = lax.all_to_all(blocks, "gy", 0, 0, tiled=True)
    total = total.astype(F32).sum(0)
    mine, other = total[: 2 * own_rows], total[2 * own_rows :]
    mine = mine.reshape(2, own_rows, chan)
    swapped = pair(pick(mine, 1 - core, 0))
    mine = pick(mine, core, 0)
    tail_in = jnp.where(core == 0, mine, swapped)
    tail_out = jnp.where(core == 0, swapped, mine)
    d_mode = other.reshape(M // ny, 2, own_rows, chan).transpose(1, 0, 2, 3)

    du_lo = jnp.where(core == 0, du_own, du_par).reshape(2 * M, half, chan)
    du_hi = jnp.where(core == 0, du_par, du_own).reshape(2 * M, half, chan)
    ret_lo = contract("myc,xm->yxc", du_lo, own_fwd)
    ret_hi = contract("myc,xm->yxc", du_hi, own_fwd)
    returned = jnp.concatenate([ret_lo, ret_hi], axis=0)
    d_inputs = (cotangent.astype(F32) + returned).astype(BF)
    scale_mlp = 1.0 / math.sqrt(lines * ny * total_x)
    scale_mode = 1.0 / math.sqrt(lines * ny)
    return (d_inputs, d_mode * scale_mode, tail_in.T * scale_mlp, tail_out * scale_mlp)


def solution(mesh):
    placed = (P("gy", "gx", None), P("gy", "gx", None), P(None, None, "gx", None), P(), P())
    return jax.shard_map(
        local,
        mesh=mesh,
        in_specs=placed,
        out_specs=(
            P("gy", "gx", None),
            P(None, "gy", "gx", None),
            P(None, ("gy", "gx")),
            P(("gy", "gx"), None),
        ),
        check_vma=False,
    )
```

time: 153 us -> 138 us (0.902)
  the two profiles are of different devices: /device:TPU:2 before, /device:TPU:1 now
where the time goes in v2:
time: 138 us; the launch traced here: 137 us
  starting transfers between devices  38.2 us (28%)
  Pallas kernels  28.7 us (21%)
  blocking collectives  24.5 us (18%)
  waiting for transfers between devices  23.8 us (17%)
  local copies, waits for them, and re-layouts  10.4 us (8%)
  other arithmetic  6.84 us (5%)
  matrix products  3.33 us (2%)
    all_to_all x1, blocking collectives, spread(): return lax.all_to_all(x, 'gx', 0, 0, tiled=True, axis_index_groups=groups)  24.5 us
    all_to_all x3, starting transfers between devices, spread(): return lax.all_to_all(x, 'gx', 0, 0, tiled=True, axis_index_groups=groups)  18.7 us
    pallas_call x1, Pallas kernels, mlp_call(): pl.pallas_call(mlp_kernel, grid=(half // block,), in_specs=[pl.BlockSpec(...  14.3 us
    all_to_all x3, waiting for transfers between devices, spread(): return lax.all_to_all(x, 'gx', 0, 0, tiled=True, axis_index_groups=groups)  13.4 us
    ppermute x8, starting transfers between devices, pair(): return lax.ppermute(x, 'gx', swap)  12.1 us
    pallas_call x1, Pallas kernels, grads_call(): pl.pallas_call(grads_kernel, grid_spec=pltpu.PrefetchScalarGridSpec(num_s...  7.59 us
    all_to_all x1, starting transfers between devices, local(): total = lax.all_to_all(blocks, 'gy', 0, 0, tiled=True)  7.28 us
    pallas_call x1, Pallas kernels, grad_act_call(): pl.pallas_call(grad_act_kernel, grid=(half // block,), in_specs=[pl.Block...  6.8 us
  transfers between devices with their start and end apart: 12, of which 8 were waited for; matrix products, arithmetic and copies ran while one was open for 9% of the time, Pallas kernels for 11%

profile of v2, /device:TPU:1, one launch (start us, length us, event | category | flops | bytes accessed | tf_op | source)
XLA Modules:
  0.0 136.7 jit_solution(12024504757465800392)
XLA Ops:
  0.7 1.2 copy-done
  1.9 3.3 %collective-permute-start = (bf16[16,64,256]{2,1,0:T(8,128)(2,1)S(1)}, bf16[16,64,256]{2,1,0:T(8,128)(2,1)S(1)}, u32[]{:S(2)}, u32[]{:S(2)}) collective-permute-start(bf16[16,64,256]{2,1,0:T(8,128)(2,1)S(1)} %dynamic-slice_bitcast_fusion.2), channel_id=1, source_target_pairs={{0,1},{1,0},{2,3},{3,2},{4,5},{5,4},{6,7},{7,6},{8,9},{9,8},{10,11... | collective-permute-start | bytes 1572872 | tf_op jit(solution)/shard_map/ppermute | solution.py:242
  5.4 0.9 copy.54
  6.5 0.3 fusion.8
  6.8 0.3 fusion.1
  7.0 0.3 copy.53
  7.3 0.9 pad_maximum_fusion.1
  8.2 6.7 %all-to-all-start = ((bf16[32,40,256]{2,1,0:T(8,128)(2,1)}), bf16[32,40,256]{2,1,0:T(8,128)(2,1)S(1)}, u32[]{:S(2)}, u32[]{:S(2)}) async-start(bf16[32,40,256]{2,1,0:T(8,128)(2,1)} %pad_maximum_fusion.1), calls=%async_computation | async-start | bytes 1310720 | tf_op jit(solution)/shard_map/all_to_all | solution.py:245
  14.9 12.8 %all-to-all-done = bf16[32,40,256]{2,1,0:T(8,128)(2,1)S(1)} async-done(((bf16[32,40,256]{2,1,0:T(8,128)(2,1)}), bf16[32,40,256]{2,1,0:T(8,128)(2,1)S(1)}, u32[]{:S(2)}, u32[]{:S(2)}) %all-to-all-start) | async-done | bytes 655392 | tf_op jit(solution)/shard_map/all_to_all | solution.py:245
  27.8 1.9 %collective-permute-start.1 = (bf16[32,2,4,256]{3,2,0,1:T(4,128)(2,1)S(1)}, bf16[32,2,4,256]{3,2,0,1:T(4,128)(2,1)S(1)}, u32[]{:S(2)}, u32[]{:S(2)}) collective-permute-start(bf16[32,2,4,256]{3,2,0,1:T(4,128)(2,1)S(1)} %copy.57), channel_id=1, source_target_pairs={{0,1},{1,0},{2,3},{3,2},{4,5},{5,4},{6,7},{7,6},{8,9},{9,8},{10,11... | collective-permute-start | bytes 393224 | tf_op jit(solution)/shard_map/ppermute | solution.py:242
  29.8 0.9 collective-permute-done.1
  31.7 0.9 broadcast_in_dim.14
  32.6 4.0 %all-to-all-start.1 = ((bf16[32,32,256]{2,1,0:T(8,128)(2,1)}), bf16[32,32,256]{2,1,0:T(8,128)(2,1)S(1)}, u32[]{:S(2)}, u32[]{:S(2)}) async-start(bf16[32,32,256]{2,1,0:T(8,128)(2,1)} %broadcast_in_dim.14), calls=%async_computation.1 | async-start | bytes 1048576 | tf_op jit(solution)/shard_map/all_to_all | solution.py:245
  36.7 1.1 dynamic-slice_bitcast_fusion
  37.8 0.4 collective-permute-start.2
  38.1 2.1 %copy.60 = bf16[1024,256]{0,1:T(8,128)(2,1)} copy(bf16[1024,256]{1,0:T(8,128)(2,1)} %param.9) | data formatting | bytes 1048576 | tf_op args[4]
  40.4 0.7 copy.64.inv_ref
  41.1 1.0 copy.63
  42.1 0.7 fusion.79.invt_ref
  42.8 6.8 %grad_act.1.ga_ref = f32[2048,1024]{1,0:T(8,128)} custom-call(bf16[16,64,256]{2,1,0:T(8,128)(2,1)} %get-tuple-element.32.own_ref, bf16[16,64,256]{2,1,0:T(8,128)(2,1)} %collective-permute-done.2.par_ref, bf16[256,1024]{1,0:T(8,128)(2,1)} %bitcast.101), custom_call_target="tpu_custom_call" | custom-call | tf_op jit(solution)/shard_map/grad_act/pallas_call | solution.py:54
  49.6 0.8 copy-done.3
  50.4 14.3 %mlp.1 = (bf16[2048,256]{1,0:T(8,128)(2,1)}, bf16[2048,1024]{1,0:T(8,128)(2,1)}, bf16[2048,1024]{1,0:T(8,128)(2,1)}, bf16[1024,256]{1,0:T(8,128)(2,1)}) custom-call(bf16[1024,256]{1,0:T(8,128)(2,1)} %bitcast.100, f32[2048,1024]{1,0:T(8,128)} %grad_act.1.ga_ref, bf16[128,64]{1,0:T(8,128)(2,1)} %copy.64.inv_ref, bf16[64,128]{1,0:T(8,128)(2,1)} %fusion.79.invt_ref, ...), custom_call_target="tpu_custom_call" | custom-call | tf_op jit(solution)/shard_map/mlp/pallas_call | solution.py:126
  64.7 8.0 %all-to-all-start.2 = ((bf16[32,32,256]{2,1,0:T(8,128)(2,1)}), bf16[32,32,256]{2,1,0:T(8,128)(2,1)S(1)}, u32[]{:S(2)}, u32[]{:S(2)}) async-start(bf16[32,32,256]{2,1,0:T(8,128)(2,1)} %bitcast.116), calls=%async_computation.2 | async-start | bytes 1048576 | tf_op jit(solution)/shard_map/all_to_all | solution.py:245
  72.7 7.6 %grads.1 = (f32[32,32,256]{2,1,0:T(8,128)}, bf16[32,32,256]{2,1,0:T(8,128)(2,1)}) custom-call(s32[1]{0:T(128)} %bitcast.25.core_ref, bf16[2048,256]{1,0:T(8,128)(2,1)} %get-tuple-element.11.hid_ref, bf16[2048,1024]{1,0:T(8,128)(2,1)} %get-tuple-element.12.dpre_ref, bf16[2048,1024]{1,0:T(8,128)(2,1)} %get-tuple-element.13.act_ref, ...), custom_call_target="tpu_custom_call" | custom-call | tf_op jit(solution)/shard_map/grads/pallas_call | solution.py:202
  80.3 0.3 collective-permute-start.3
  80.6 0.2 collective-permute-start.4
  80.8 1.6 %collective-permute-done.3 = bf16[32,32,256]{2,1,0:T(8,128)(2,1)S(1)} collective-permute-done((bf16[32,32,256]{2,1,0:T(8,128)(2,1)}, bf16[32,32,256]{2,1,0:T(8,128)(2,1)S(1)}, u32[]{:S(2)}, u32[]{:S(2)}) %collective-permute-start.3) | collective-permute-done | bytes 524320 | tf_op jit(solution)/shard_map/ppermute | solution.py:242
  82.5 1.4 %add_convert_fusion = bf16[32,32,256]{2,1,0:T(8,128)(2,1)S(1)} fusion(f32[32,32,256]{2,1,0:T(8,128)} %get-tuple-element.14, bf16[32,32,256]{2,1,0:T(8,128)(2,1)S(1)} %collective-permute-done.3), kind=kLoop, calls=%fused_computation.19 | loop fusion | flops 786432 | bytes 2097152 | tf_op jit(solution)/shard_map/convert_element_type | solution.py:296
  83.9 0.6 all-to-all-done.2
  85.3 1.5 %collective-permute-start.5 = (bf16[2,16,256]{2,1,0:T(8,128)(2,1)S(1)}, bf16[2,16,256]{2,1,0:T(8,128)(2,1)S(1)}, u32[]{:S(2)}, u32[]{:S(2)}) collective-permute-start(bf16[2,16,256]{2,1,0:T(8,128)(2,1)S(1)} %bitcast.111), channel_id=1, source_target_pairs={{0,1},{1,0},{2,3},{3,2},{4,5},{5,4},{6,7},{7,6},{8,9},{9,8},{10,11... | collective-permute-start | bytes 49160 | tf_op jit(solution)/shard_map/ppermute | solution.py:242
  86.7 0.8 collective-permute-done.5
  87.6 0.2 fusion.51
  87.8 0.2 fusion.3
  88.0 0.2 fusion.53
  88.3 0.2 fusion.2
  88.8 24.5 %all_to_all.25 = bf16[32,72,256]{2,1,0:T(8,128)(2,1)S(1)} all-to-all(bf16[32,72,256]{2,1,0:T(8,128)(2,1)S(1)} %pad_maximum_fusion), channel_id=1, replica_groups={{0,2,4,6,8,10,12,14,16,18,20,22,24,26,28,30,32,34,36,38,40,42,44,46,48,..., dimensions={0} | all-to-all | bytes 2359296 | tf_op jit(solution)/shard_map/all_to_all | solution.py:245
  113.3 1.9 %collective-permute-start.6 = (bf16[32,32,256]{2,1,0:T(8,128)(2,1)S(1)}, bf16[32,32,256]{2,1,0:T(8,128)(2,1)S(1)}, u32[]{:S(2)}, u32[]{:S(2)}) collective-permute-start(bf16[32,32,256]{2,1,0:T(8,128)(2,1)S(1)} %slice.93), channel_id=1, source_target_pairs={{0,1},{1,0},{2,3},{3,2},{4,5},{5,4},{6,7},{7,6},{8,9},{9,8},{10,11... | collective-permute-start | bytes 1572872 | tf_op jit(solution)/shard_map/ppermute | solution.py:242
  115.2 1.5 %collective-permute-done.6 = bf16[32,32,256]{2,1,0:T(8,128)(2,1)S(1)} collective-permute-done((bf16[32,32,256]{2,1,0:T(8,128)(2,1)S(1)}, bf16[32,32,256]{2,1,0:T(8,128)(2,1)S(1)}, u32[]{:S(2)}, u32[]{:S(2)}) %collective-permute-start.6) | collective-permute-done | bytes 524320 | tf_op jit(solution)/shard_map/ppermute | solution.py:242
  116.7 0.3 broadcast_select_fusion.1
  117.0 0.7 pad_maximum_fusion.2
  117.7 7.3 %all-to-all-start.4 = ((bf16[4,72,256]{2,1,0:T(8,128)(2,1)}), bf16[4,72,256]{2,1,0:T(8,128)(2,1)S(1)}, u32[]{:S(2)}, u32[]{:S(2)}) async-start(bf16[4,72,256]{2,1,0:T(8,128)(2,1)} %pad_maximum_fusion.2), calls=%async_computation.4 | async-start | bytes 294912 | tf_op jit(solution)/shard_map/all_to_all | solution.py:306
  125.0 0.3 convolution_bitcast_fusion.1
  125.3 0.3 convolution_bitcast_fusion
  125.7 1.4 %fusion = bf16[32,64,256]{2,1,0:T(8,128)(2,1)} fusion(f32[16,64,256]{2,1,0:T(8,128)S(1)} %convolution_bitcast_fusion, f32[16,64,256]{2,1,0:T(8,128)S(1)} %convolution_bitcast_fusion.1, bf16[32,64,256]{2,1,0:T(8,128)(2,1)S(1)} %copy-done.1), kind=kLoop, calls=%fused_computation.1 | loop fusion | flops 2097152 | bytes 4194304 | tf_op jit(solution)/shard_map/convert_element_type | solution.py:321
  127.0 5.4 %all-to-all-done.4 = bf16[4,72,256]{2,1,0:T(8,128)(2,1)S(1)} async-done(((bf16[4,72,256]{2,1,0:T(8,128)(2,1)}), bf16[4,72,256]{2,1,0:T(8,128)(2,1)S(1)}, u32[]{:S(2)}, u32[]{:S(2)}) %all-to-all-start.4) | async-done | bytes 147488 | tf_op jit(solution)/shard_map/all_to_all | solution.py:306
  132.5 2.8 %collective-permute-start.7 = (f32[4,256]{1,0:T(4,128)S(1)}, f32[4,256]{1,0:T(4,128)S(1)}, u32[]{:S(2)}, u32[]{:S(2)}) collective-permute-start(f32[4,256]{1,0:T(4,128)S(1)} %dynamic-slice_bitcast_fusion.3), channel_id=1, source_target_pairs={{0,1},{1,0},{2,3},{3,2},{4,5},{5,4},{6,7},{7,6},{8,9},{9,8},{10,11... | collective-permute-start | bytes 12296 | tf_op jit(solution)/shard_map/ppermute | solution.py:242
  135.3 0.6 copy.70
  136.1 0.6 fusion.50
  (59 shorter events, 3.1 us)
Async XLA Ops:
  0.6 1.2 copy-start
  1.9 4.8 %collective-permute-start = (bf16[16,64,256]{2,1,0:T(8,128)(2,1)S(1)}, bf16[16,64,256]{2,1,0:T(8,128)(2,1)S(1)}, u32[]{:S(2)}, u32[]{:S(2)}) collective-permute-start(bf16[16,64,256]{2,1,0:T(8,128)(2,1)S(1)} %dynamic-slice_bitcast_fusion.2), channel_id=1, source_target_pairs={{0,1},{1,0},{2,3},{3,2},{4,5},{5,4},{6,7},{7,6},{8,9},{9,8},{10,11... | collective-permute-start | bytes 1572872 | tf_op jit(solution)/shard_map/ppermute | solution.py:242
  8.2 19.5 %all-to-all-start = ((bf16[32,40,256]{2,1,0:T(8,128)(2,1)}), bf16[32,40,256]{2,1,0:T(8,128)(2,1)S(1)}, u32[]{:S(2)}, u32[]{:S(2)}) async-start(bf16[32,40,256]{2,1,0:T(8,128)(2,1)} %pad_maximum_fusion.1), calls=%async_computation | async-start | bytes 1310720 | tf_op jit(solution)/shard_map/all_to_all | solution.py:245
  27.8 2.9 %collective-permute-start.1 = (bf16[32,2,4,256]{3,2,0,1:T(4,128)(2,1)S(1)}, bf16[32,2,4,256]{3,2,0,1:T(4,128)(2,1)S(1)}, u32[]{:S(2)}, u32[]{:S(2)}) collective-permute-start(bf16[32,2,4,256]{3,2,0,1:T(4,128)(2,1)S(1)} %copy.57), channel_id=1, source_target_pairs={{0,1},{1,0},{2,3},{3,2},{4,5},{5,4},{6,7},{7,6},{8,9},{9,8},{10,11... | collective-permute-start | bytes 393224 | tf_op jit(solution)/shard_map/ppermute | solution.py:242
  29.8 6.9 %copy-start.1 = (bf16[32,64,256]{2,1,0:T(8,128)(2,1)S(1)}, bf16[32,64,256]{2,1,0:T(8,128)(2,1)}, u32[]{:S(2)}) copy-start(bf16[32,64,256]{2,1,0:T(8,128)(2,1)} %param.6) | copy-start | bytes 3145732
  32.6 8.5 %copy-start.2 = (bf16[256,1024]{1,0:T(8,128)(2,1)S(1)}, bf16[256,1024]{1,0:T(8,128)(2,1)}, u32[]{:S(2)}) copy-start(bf16[256,1024]{1,0:T(8,128)(2,1)} %wi_ref.1) | copy-start | bytes 1572868
  32.6 17.0 %all-to-all-start.1 = ((bf16[32,32,256]{2,1,0:T(8,128)(2,1)}), bf16[32,32,256]{2,1,0:T(8,128)(2,1)S(1)}, u32[]{:S(2)}, u32[]{:S(2)}) async-start(bf16[32,32,256]{2,1,0:T(8,128)(2,1)} %broadcast_in_dim.14), calls=%async_computation.1 | async-start | bytes 1048576 | tf_op jit(solution)/shard_map/all_to_all | solution.py:245
  37.8 5.0 %collective-permute-start.2 = (bf16[16,64,256]{2,1,0:T(8,128)(2,1)}, bf16[16,64,256]{2,1,0:T(8,128)(2,1)}, u32[]{:S(2)}, u32[]{:S(2)}) collective-permute-start(bf16[16,64,256]{2,1,0:T(8,128)(2,1)} %get-tuple-element.31), channel_id=1, source_target_pairs={{0,1},{1,0},{2,3},{3,2},{4,5},{5,4},{6,7},{7,6},{8,9},{9,8},{10,11... | collective-permute-start | bytes 1572872 | tf_op jit(solution)/shard_map/ppermute | solution.py:242
  49.6 0.8 copy-start.3
  64.7 19.8 %all-to-all-start.2 = ((bf16[32,32,256]{2,1,0:T(8,128)(2,1)}), bf16[32,32,256]{2,1,0:T(8,128)(2,1)S(1)}, u32[]{:S(2)}, u32[]{:S(2)}) async-start(bf16[32,32,256]{2,1,0:T(8,128)(2,1)} %bitcast.116), calls=%async_computation.2 | async-start | bytes 1048576 | tf_op jit(solution)/shard_map/all_to_all | solution.py:245
  80.3 2.1 %collective-permute-start.3 = (bf16[32,32,256]{2,1,0:T(8,128)(2,1)}, bf16[32,32,256]{2,1,0:T(8,128)(2,1)S(1)}, u32[]{:S(2)}, u32[]{:S(2)}) collective-permute-start(bf16[32,32,256]{2,1,0:T(8,128)(2,1)} %get-tuple-element.15), channel_id=1, source_target_pairs={{0,1},{1,0},{2,3},{3,2},{4,5},{5,4},{6,7},{7,6},{8,9},{9,8},{10,11... | collective-permute-start | bytes 1572872 | tf_op jit(solution)/shard_map/ppermute | solution.py:242
  80.6 6.1 %collective-permute-start.4 = (bf16[2,16,256]{2,1,0:T(8,128)(2,1)S(1)}, bf16[2,16,256]{2,1,0:T(8,128)(2,1)S(1)}, u32[]{:S(2)}, u32[]{:S(2)}) collective-permute-start(bf16[2,16,256]{2,1,0:T(8,128)(2,1)S(1)} %bitcast.106), channel_id=1, source_target_pairs={{0,1},{1,0},{2,3},{3,2},{4,5},{5,4},{6,7},{7,6},{8,9},{9,8},{10,11... | collective-permute-start | bytes 49160 | tf_op jit(solution)/shard_map/ppermute | solution.py:242
  85.3 2.3 %collective-permute-start.5 = (bf16[2,16,256]{2,1,0:T(8,128)(2,1)S(1)}, bf16[2,16,256]{2,1,0:T(8,128)(2,1)S(1)}, u32[]{:S(2)}, u32[]{:S(2)}) collective-permute-start(bf16[2,16,256]{2,1,0:T(8,128)(2,1)S(1)} %bitcast.111), channel_id=1, source_target_pairs={{0,1},{1,0},{2,3},{3,2},{4,5},{5,4},{6,7},{7,6},{8,9},{9,8},{10,11... | collective-permute-start | bytes 49160 | tf_op jit(solution)/shard_map/ppermute | solution.py:242
  113.3 3.4 %collective-permute-start.6 = (bf16[32,32,256]{2,1,0:T(8,128)(2,1)S(1)}, bf16[32,32,256]{2,1,0:T(8,128)(2,1)S(1)}, u32[]{:S(2)}, u32[]{:S(2)}) collective-permute-start(bf16[32,32,256]{2,1,0:T(8,128)(2,1)S(1)} %slice.93), channel_id=1, source_target_pairs={{0,1},{1,0},{2,3},{3,2},{4,5},{5,4},{6,7},{7,6},{8,9},{9,8},{10,11... | collective-permute-start | bytes 1572872 | tf_op jit(solution)/shard_map/ppermute | solution.py:242
  117.7 14.7 %all-to-all-start.4 = ((bf16[4,72,256]{2,1,0:T(8,128)(2,1)}), bf16[4,72,256]{2,1,0:T(8,128)(2,1)S(1)}, u32[]{:S(2)}, u32[]{:S(2)}) async-start(bf16[4,72,256]{2,1,0:T(8,128)(2,1)} %pad_maximum_fusion.2), calls=%async_computation.4 | async-start | bytes 294912 | tf_op jit(solution)/shard_map/all_to_all | solution.py:306
  132.5 3.6 %collective-permute-start.7 = (f32[4,256]{1,0:T(4,128)S(1)}, f32[4,256]{1,0:T(4,128)S(1)}, u32[]{:S(2)}, u32[]{:S(2)}) collective-permute-start(f32[4,256]{1,0:T(4,128)S(1)} %dynamic-slice_bitcast_fusion.3), channel_id=1, source_target_pairs={{0,1},{1,0},{2,3},{3,2},{4,5},{5,4},{6,7},{7,6},{8,9},{9,8},{10,11... | collective-permute-start | bytes 12296 | tf_op jit(solution)/shard_map/ppermute | solution.py:242

commit v3 on v2

v3 whole, which is shorter than its diff:
```python
import math

import jax
import jax.numpy as jnp
from jax import lax
from jax.experimental import pallas as pl
from jax.experimental.pallas import tpu as pltpu
from jax.sharding import PartitionSpec as P

M = 32
LANES = 128
BF = jnp.bfloat16
F32 = jnp.float32


def bases(positions, length, modes):
    order = jnp.arange(modes, dtype=jnp.int32)
    phase = positions[:, None] * order[None, :] % length
    angle = phase.astype(F32) * (2.0 * math.pi / length)
    factor = 1.0 / math.sqrt(length)
    cosine = jnp.cos(angle) * factor
    sine = jnp.sin(angle) * factor
    weight = jnp.where(order == 0, 1.0, 2.0).astype(F32)
    forward = jnp.stack([cosine, -sine], axis=2).astype(BF)
    inverse = jnp.stack([cosine * weight, -sine * weight], axis=2).astype(BF)
    size = positions.shape[0]
    return forward.reshape(size, 2 * modes), inverse.reshape(size, 2 * modes)


def contract(form, left, right):
    return jnp.einsum(form, left, right, preferred_element_type=F32)


def dot(left, right):
    return jnp.dot(left, right, preferred_element_type=F32)


def rows_dot(left, right):
    return lax.dot_general(left, right, (((0,), (0,)), ((), ())), preferred_element_type=F32)


GELU_A = math.sqrt(2.0 / math.pi)
GELU_B = 0.044715 * GELU_A


def mlp_kernel(
    mix_ref, own_ref, par_ref, inv_ref, invt_ref, wi_ref, wit_ref, wot_ref,
    hid_ref, act_ref, dpre_ref, part_ref,
    mix_lo, mix_hi, part_lo, part_hi, pre_s, ga_s, dh_s,
):
    i = pl.program_id(0)
    block, cols, chan = own_ref.shape
    modes = inv_ref.shape[1]
    half = mix_ref.shape[0] // modes
    side = block * cols
    chunk = 32

    @pl.when(i == 0)
    def _():
        mix_lo[...] = mix_ref[:, :LANES].astype(F32)
        mix_hi[...] = mix_ref[:, LANES:].astype(F32)

    for b in range(block):
        lines = pl.ds(i * block + b, modes, stride=half)
        table = jnp.concatenate([mix_lo[lines, :], mix_hi[lines, :]], axis=1).astype(BF)
        h = dot(inv_ref[...], table).astype(BF)
        hid_ref[b * cols : (b + 1) * cols, :] = h[:cols]
        hid_ref[side + b * cols : side + (b + 1) * cols, :] = h[cols:]
    for k, ref in ((0, own_ref), (1, par_ref)):
        rows = slice(k * side, (k + 1) * side)
        pre_s[k] = dot(hid_ref[rows, :], wi_ref[...])
        ga_s[k] = dot(ref[...].reshape(side, chan), wot_ref[...])
        for r in range(0, side, chunk):
            p = pre_s[k, r : r + chunk, :]
            g = ga_s[k, r : r + chunk, :]
            sq = p * p
            t = 0.5 * jnp.tanh(p * (GELU_A + GELU_B * sq))
            s = 0.5 + t
            a = p * s
            slope = s + (a * (0.5 - t)) * (2.0 * GELU_A + (6.0 * GELU_B) * sq)
            there = slice(k * side + r, k * side + r + chunk)
            act_ref[there, :] = a.astype(BF)
            dpre_ref[there, :] = (g * slope).astype(BF)
        dh_s[rows, :] = dot(dpre_ref[rows, :], wit_ref[...])
    for b in range(block):
        lines = pl.ds(i * block + b, modes, stride=half)
        mine = dh_s[b * cols : (b + 1) * cols, :]
        other = dh_s[side + b * cols : side + (b + 1) * cols, :]
        sums = dot(invt_ref[...], jnp.concatenate([mine, other], axis=0).astype(BF))
        part_lo[lines, :] = sums[:, :LANES]
        part_hi[lines, :] = sums[:, LANES:]

    @pl.when(i == pl.num_programs(0) - 1)
    def _():
        part_ref[:, :LANES] = part_lo[...].astype(BF)
        part_ref[:, LANES:] = part_hi[...].astype(BF)


def mlp_call(mix, own, par, inv, w_in, w_out_t, block=4):
    half, cols, chan = own.shape
    modes = inv.shape[1]
    width = w_in.shape[1]
    rows = 2 * block * cols
    whole = lambda i: (0, 0)
    step = lambda i: (i, 0)
    line = lambda i: (i, 0, 0)
    return pl.pallas_call(
        mlp_kernel,
        grid=(half // block,),
        in_specs=[
            pl.BlockSpec((modes * half, chan), whole),
            pl.BlockSpec((block, cols, chan), line),
            pl.BlockSpec((block, cols, chan), line),
            pl.BlockSpec((2 * cols, modes), whole),
            pl.BlockSpec((modes, 2 * cols), whole),
            pl.BlockSpec((chan, width), whole),
            pl.BlockSpec((width, chan), whole),
            pl.BlockSpec((chan, width), whole),
        ],
        out_specs=[
            pl.BlockSpec((rows, chan), step),
            pl.BlockSpec((rows, width), step),
            pl.BlockSpec((rows, width), step),
            pl.BlockSpec((modes * half, chan), whole),
        ],
        out_shape=[
            pltpu.HBM((2 * half * cols, chan), BF),
            pltpu.HBM((2 * half * cols, width), BF),
            pltpu.HBM((2 * half * cols, width), BF),
            pltpu.HBM((modes * half, chan), BF),
        ],
        scratch_shapes=[pltpu.VMEM((modes * half, LANES), F32)] * 4
        + [pltpu.VMEM((2, block * cols, width), F32)] * 2
        + [pltpu.VMEM((rows, chan), F32)],
        compiler_params=pltpu.CompilerParams(vmem_limit_bytes=30 << 20),
        name="mlp",
    )(mix, own, par, inv, inv.T, w_in, w_in.T, w_out_t)


def grads_kernel(core_ref, hid_ref, dpre_ref, act_ref, own_ref, par_ref, keep_ref, send_ref, acc_in, acc_out):
    i = pl.program_id(0)
    block, cols, _ = own_ref.shape
    chips, kept, _ = keep_ref.shape
    groups = kept // 8

    @pl.when(i == 0)
    def _():
        acc_in[...] = jnp.zeros_like(acc_in)
        acc_out[...] = jnp.zeros_like(acc_out)

    acc_in[...] += rows_dot(hid_ref[...], dpre_ref[...])
    flat = (block * cols, own_ref.shape[2])
    cot = jnp.concatenate([own_ref[...].reshape(flat), par_ref[...].reshape(flat)], axis=0)
    acc_out[...] += rows_dot(cot, act_ref[...])

    def store(ref, acc):
        full = acc[...].T
        for t in range(chips):
            for g in range(groups):
                top = (g * chips + t) * 8
                if ref.dtype == F32:
                    ref[t, g * 8 : (g + 1) * 8, :] = full[top : top + 8]
            if ref.dtype != F32:
                ref[t] = jnp.concatenate(
                    [full[(g * chips + t) * 8 : (g * chips + t) * 8 + 8] for g in range(groups)], axis=0
                ).astype(ref.dtype)

    last = i == pl.num_programs(0) - 1

    @pl.when(last & (core_ref[0] == 0))
    def _():
        store(keep_ref, acc_in)
        store(send_ref, acc_out)

    @pl.when(last & (core_ref[0] != 0))
    def _():
        store(keep_ref, acc_out)
        store(send_ref, acc_in)


def in_hbm(x):
    return pltpu.with_memory_space_constraint(x, pltpu.HBM)


def grads_call(core, hidden, d_pre, act, own, par, chips, block=4):
    half, cols, chan = own.shape
    width = act.shape[1]
    rows = block * 2 * cols
    kept = width // chips
    step = lambda i, c: (i, 0)
    line = lambda i, c: (i, 0, 0)
    whole = lambda i, c: (0, 0, 0)
    return pl.pallas_call(
        grads_kernel,
        grid_spec=pltpu.PrefetchScalarGridSpec(
            num_scalar_prefetch=1,
            grid=(half // block,),
            in_specs=[
                pl.BlockSpec((rows, chan), step),
                pl.BlockSpec((rows, width), step),
                pl.BlockSpec((rows, width), step),
                pl.BlockSpec((block, cols, chan), line),
                pl.BlockSpec((block, cols, chan), line),
            ],
            out_specs=[
                pl.BlockSpec((chips, kept, chan), whole),
                pl.BlockSpec((chips, kept, chan), whole),
            ],
            scratch_shapes=[pltpu.VMEM((chan, width), F32), pltpu.VMEM((chan, width), F32)],
        ),
        out_shape=[
            jax.ShapeDtypeStruct((chips, kept, chan), F32),
            jax.ShapeDtypeStruct((chips, kept, chan), BF),
        ],
        compiler_params=pltpu.CompilerParams(vmem_limit_bytes=26 << 20),
        name="grads",
    )(core.reshape(1), in_hbm(hidden), in_hbm(d_pre), in_hbm(act), own, par)


def sum_kernel(recv_ref, out_ref):
    total = recv_ref[0].astype(F32)
    for t in range(1, recv_ref.shape[0]):
        total = total + recv_ref[t].astype(F32)
    out_ref[...] = total.astype(BF)


def sum_call(recv, rows):
    chips, _, chan = recv.shape
    return pl.pallas_call(
        sum_kernel,
        grid=(1,),
        in_specs=[pl.BlockSpec((chips, rows, chan), lambda i: (0, 0, 0))],
        out_specs=pl.BlockSpec((rows, chan), lambda i: (0, 0)),
        out_shape=jax.ShapeDtypeStruct((rows, chan), BF),
        compiler_params=pltpu.CompilerParams(vmem_limit_bytes=6 << 20),
        name="sum_parts",
    )(recv)


def by_half(low, high):
    row = lax.broadcasted_iota(jnp.int32, low.shape, 1)
    return jnp.where(row < 4, low, high)


def mix_kernel(core_ref, u_ref, own_ref, par_ref, out_ref, re_ref, im_ref):
    even = core_ref[0] == 0
    own = own_ref[...].astype(F32)
    par = par_ref[...].astype(F32)
    first = jnp.where(even, own, par)
    second = jnp.where(even, par, own)
    chan = re_ref.shape[0]
    re_ref[...] = by_half(first, pltpu.roll(second, 4, 1)).reshape(chan, chan).astype(BF)
    im_ref[...] = by_half(pltpu.roll(first, 4, 1), second).reshape(chan, chan).astype(BF)
    half = u_ref.shape[0] // 2
    by_re = dot(u_ref[...], re_ref[...])
    by_im = dot(u_ref[...], im_ref[...])
    vr = by_re[:half] - by_im[half:]
    vi = by_re[half:] + by_im[:half]
    mixed = jnp.concatenate([vr, vi], axis=0).astype(BF)
    for t in range(out_ref.shape[0]):
        out_ref[t] = mixed


def mix_call(core, u, own, par):
    chips, _, chan = own.shape
    vmem = pl.BlockSpec(memory_space=pltpu.VMEM)
    return pl.pallas_call(
        mix_kernel,
        in_specs=[pl.BlockSpec(memory_space=pltpu.SMEM), vmem, vmem, vmem],
        out_specs=[vmem, vmem, vmem],
        out_shape=[
            pltpu.HBM((chips, u.shape[0], chan), BF),
            pltpu.HBM((chan, chan), BF),
            pltpu.HBM((chan, chan), BF),
        ],
        compiler_params=pltpu.CompilerParams(vmem_limit_bytes=8 << 20),
        name="mix",
    )(core.reshape(1), u, own, par)


def last_kernel(core_ref, u_ref, upar_ref, d_ref, dpar_ref, re_ref, im_ref, gown_ref, gpar_ref, out_ref, du_ref):
    even = core_ref[0] == 0
    both = d_ref.shape[0]
    half = both // 2
    chips, kept, chan = gown_ref.shape
    across = (((1,), (1,)), ((), ()))
    by_re = lax.dot_general(d_ref[...], re_ref[...], across, preferred_element_type=F32)
    by_im = lax.dot_general(d_ref[...], im_ref[...], across, preferred_element_type=F32)
    du_re = by_re[:half] + by_im[half:]
    du_im = by_re[half:] - by_im[:half]
    du = jnp.concatenate([du_re, du_im], axis=0).astype(BF)
    u_re = jnp.concatenate([u_ref[:half], upar_ref[:half]], axis=0)
    u_im = jnp.concatenate([u_ref[half:], upar_ref[half:]], axis=0)
    d_re = jnp.concatenate([d_ref[:half], dpar_ref[:half]], axis=0)
    d_im = jnp.concatenate([d_ref[half:], dpar_ref[half:]], axis=0)
    u_all = jnp.concatenate([u_re, u_im], axis=0)
    g_re = rows_dot(u_all, jnp.concatenate([d_re, d_im], axis=0)).reshape(chips, 8, chan)
    g_im = rows_dot(u_all, jnp.concatenate([d_im, -d_re], axis=0)).reshape(chips, 8, chan)
    low = jnp.where(even, g_re, pltpu.roll(g_re, 4, 1))
    high = jnp.where(even, pltpu.roll(g_im, 4, 1), g_im)
    out_ref[:, kept:, :] = by_half(low, high).astype(BF)
    for t in range(chips):
        du_ref[t] = du
        out_ref[t, :kept, :] = (gown_ref[t] + gpar_ref[t].astype(F32)).astype(BF)


def last_call(core, u, u_par, d, d_par, w_re, w_im, g_own, g_par):
    chips, kept, chan = g_own.shape
    vmem = pl.BlockSpec(memory_space=pltpu.VMEM)
    return pl.pallas_call(
        last_kernel,
        in_specs=[pl.BlockSpec(memory_space=pltpu.SMEM)] + [vmem] * 8,
        out_specs=[vmem, vmem],
        out_shape=[
            jax.ShapeDtypeStruct((chips, kept + 8, chan), BF),
            jax.ShapeDtypeStruct((chips, d.shape[0], chan), BF),
        ],
        compiler_params=pltpu.CompilerParams(vmem_limit_bytes=14 << 20),
        name="last",
    )(core.reshape(1), u, u_par, d, d_par, w_re, w_im, g_own, g_par)


def lines_kernel(recv_ref, out_ref):
    groups, _, _ = out_ref.shape
    chips, kept, _ = recv_ref.shape
    own = kept - 8
    total = recv_ref[0, :own, :].astype(F32)
    for t in range(1, chips):
        total = total + recv_ref[t, :own, :].astype(F32)
    per = chips // groups
    for g in range(groups):
        parts = [total[8 * g : 8 * g + 8]]
        parts += [recv_ref[t, own:, :].astype(F32) for t in range(g * per, (g + 1) * per)]
        out_ref[g] = jnp.concatenate(parts, axis=0).astype(BF)


def lines_call(recv, groups):
    chips, _, chan = recv.shape
    per = chips // groups
    vmem = pl.BlockSpec(memory_space=pltpu.VMEM)
    return pl.pallas_call(
        lines_kernel,
        in_specs=[vmem],
        out_specs=vmem,
        out_shape=jax.ShapeDtypeStruct((groups, 8 + 8 * per, chan), BF),
        compiler_params=pltpu.CompilerParams(vmem_limit_bytes=8 << 20),
        name="lines_rows",
    )(recv)


def local(inputs, cotangent, mode_weight, w_in, w_out):
    lines, cols, chan = inputs.shape
    nx = lax.axis_size("gx")
    ny = lax.axis_size("gy")
    chips = nx // 2
    total_x = cols * nx
    half = lines // 2
    own_rows = chan // nx
    me = lax.axis_index("gx")
    gy = lax.axis_index("gy")
    core = me % 2
    groups = [[2 * t + c for t in range(chips)] for c in range(2)]
    swap = [(i, i ^ 1) for i in range(nx)]

    def pair(x):
        return lax.ppermute(x, "gx", swap)

    def spread(x):
        return lax.all_to_all(x, "gx", 0, 0, tiled=True, axis_index_groups=groups)

    def pick(x, which, axis):
        return lax.dynamic_index_in_dim(x, which, axis, keepdims=False)

    inp2 = inputs.reshape(2, half, cols, chan)
    cot2 = cotangent.reshape(2, half, cols, chan)
    in_par = pair(pick(inp2, 1 - core, 0))
    cot_par = pair(pick(cot2, 1 - core, 0))
    in_own = pick(inp2, core, 0)
    cot_own = pick(cot2, core, 0)
    steps = jnp.arange(cols, dtype=jnp.int32)
    own_fwd, own_inv = bases(me * cols + steps, total_x, M)
    par_fwd, par_inv = bases((me ^ 1) * cols + steps, total_x, M)
    inv = jnp.concatenate([own_inv, par_inv], axis=0)

    spec_part = contract("yxc,xm->myc", in_own, own_fwd) + contract("yxc,xm->myc", in_par, par_fwd)
    spec_part = spec_part.astype(BF).reshape(chips, 2 * half, chan)
    weight_rows = mode_weight.transpose(1, 0, 2, 3).reshape(M, 2 * own_rows, chan)
    recv = spread(jnp.concatenate([spec_part, weight_rows], axis=1))
    both = 2 * half
    w_mine = recv[:, both:]
    w_par = pair(w_mine)
    spec = sum_call(recv, both)
    sent, w_re, w_im = mix_call(core, spec, w_mine, w_par)
    mixed = spread(sent)
    spec_par = pair(spec)
    hidden, act, d_pre, d_part = mlp_call(
        mixed.reshape(2 * M * half, chan), cot_own, cot_par, inv, w_in, w_out.T
    )
    dv = spread(d_part.reshape(chips, both, chan))
    g_own, g_send = grads_call(core, hidden, d_pre, act, cot_own, cot_par, chips)
    g_par = pair(g_send)
    dv = sum_call(dv, both)
    dv_par = pair(dv)
    sent, du = last_call(core, spec, spec_par, dv, dv_par, w_re, w_im, g_own, g_par)
    recv = spread(sent)
    recv, du = lax.optimization_barrier((recv, du))
    du_own = spread(du)
    du_par = pair(du_own)
    blocks = lines_call(recv, ny)
    total = pick(blocks, gy, 0).astype(F32)
    for d in range(1, ny):
        sent = pick(blocks, (gy + d) % ny, 0)
        moved = lax.ppermute(sent, "gy", [(i, (i + d) % ny) for i in range(ny)])
        total = total + moved.astype(F32)
    mine, other = total[: 2 * own_rows], total[2 * own_rows :]
    mine = mine.reshape(2, own_rows, chan)
    swapped = pair(pick(mine, 1 - core, 0))
    mine = pick(mine, core, 0)
    tail_in = jnp.where(core == 0, mine, swapped)
    tail_out = jnp.where(core == 0, swapped, mine)
    d_mode = other.reshape(M // ny, 2, own_rows, chan).transpose(1, 0, 2, 3)

    du_lo = jnp.where(core == 0, du_own, du_par).reshape(2 * M, half, chan)
    du_hi = jnp.where(core == 0, du_par, du_own).reshape(2 * M, half, chan)
    ret_lo = contract("myc,xm->yxc", du_lo, own_fwd)
    ret_hi = contract("myc,xm->yxc", du_hi, own_fwd)
    returned = jnp.concatenate([ret_lo, ret_hi], axis=0)
    d_inputs = (cotangent.astype(F32) + returned).astype(BF)
    scale_mlp = 1.0 / math.sqrt(lines * ny * total_x)
    scale_mode = 1.0 / math.sqrt(lines * ny)
    return (d_inputs, d_mode * scale_mode, tail_in.T * scale_mlp, tail_out * scale_mlp)


def solution(mesh):
    placed = (P("gy", "gx", None), P("gy", "gx", None), P(None, None, "gx", None), P(), P())
    return jax.shard_map(
        local,
        mesh=mesh,
        in_specs=placed,
        out_specs=(
            P("gy", "gx", None),
            P(None, "gy", "gx", None),
            P(None, ("gy", "gx")),
            P(("gy", "gx"), None),
        ),
        check_vma=False,
    )
```

time: 138 us -> 120 us (0.87)
  the two profiles are of different devices: /device:TPU:1 before, /device:TPU:2 now
where the time goes in v3:
time: 120 us; the launch traced here: 118 us
  blocking collectives  39.8 us (33%)
  starting transfers between devices  27.1 us (23%)
  Pallas kernels  20.3 us (17%)
  waiting for transfers between devices  16.9 us (14%)
  local copies, waits for them, and re-layouts  9.36 us (8%)
  other arithmetic  2.46 us (2%)
  matrix products  1.22 us (1%)
    all_to_all x2, blocking collectives, spread(): return lax.all_to_all(x, 'gx', 0, 0, tiled=True, axis_index_groups=groups)  39.8 us
    all_to_all x3, starting transfers between devices, spread(): return lax.all_to_all(x, 'gx', 0, 0, tiled=True, axis_index_groups=groups)  15 us
    ppermute x3, starting transfers between devices, local(): moved = lax.ppermute(sent, 'gy', [(i, (i + d) % ny) for i in range(ny)])  10.7 us
    pallas_call x1, Pallas kernels, mlp_call(): pl.pallas_call(mlp_kernel, grid=(half // block,), in_specs=[pl.BlockSpec(...  10.7 us
    all_to_all x3, waiting for transfers between devices, spread(): return lax.all_to_all(x, 'gx', 0, 0, tiled=True, axis_index_groups=groups)  9.82 us
    pallas_call x1, Pallas kernels, grads_call(): pl.pallas_call(grads_kernel, grid_spec=pltpu.PrefetchScalarGridSpec(num_s...  7.19 us
    unnamed x18, local copies, waits for them, and re-layouts  5.07 us
    ppermute x3, waiting for transfers between devices, local(): moved = lax.ppermute(sent, 'gy', [(i, (i + d) % ny) for i in range(ny)])  3.63 us
  transfers between devices with their start and end apart: 14, of which 8 were waited for; matrix products, arithmetic and copies ran while one was open for 6% of the time, Pallas kernels for 6%

profile of v3, /device:TPU:2, one launch (start us, length us, event | category | flops | bytes accessed | tf_op | source)
XLA Modules:
  0.0 118.2 jit_solution(7887510686527143616)
XLA Ops:
  0.7 1.2 %copy-done = bf16[32,64,256]{2,1,0:T(8,128)(2,1)S(1)} copy-done((bf16[32,64,256]{2,1,0:T(8,128)(2,1)S(1)}, bf16[32,64,256]{2,1,0:T(8,128)(2,1)}, u32[]{:S(2)}) %copy-start) | copy-done | bytes 1048600
  1.9 0.1 collective-permute-start
  2.0 0.2 multiply_convert_fusion.3
  2.3 1.0 copy.34
  3.3 0.3 fusion.2
  3.6 0.3 collective-permute-done
  3.9 0.3 fusion.1
  4.2 0.3 copy.33
  4.6 21.5 %all_to_all.25.recv_ref = bf16[32,40,256]{2,1,0:T(8,128)(2,1)S(1)} all-to-all(bf16[32,40,256]{2,1,0:T(8,128)(2,1)S(1)} %pad_maximum_fusion), channel_id=1, replica_groups={{0,2,4,6,8,10,12,14,16,18,20,22,24,26,28,30,32,34,36,38,40,42,44,46,48,..., dimensions={0} | all-to-all | bytes 1310720 | tf_op jit(solution)/shard_map/all_to_all | solution.py:369
  26.1 0.1 collective-permute-start.2
  26.2 0.1 sum_parts.2.u_ref
  26.3 1.3 %collective-permute-done.2.par_ref = bf16[32,8,256]{2,1,0:T(8,128)(2,1)S(1)} collective-permute-done((bf16[32,8,256]{2,1,0:T(8,128)(2,1)S(1)}, bf16[32,8,256]{2,1,0:T(8,128)(2,1)S(1)}, u32[]{:S(2)}, u32[]{:S(2)}) %collective-permute-start.2) | collective-permute-done | bytes 131104 | tf_op jit(solution)/shard_map/ppermute | solution.py:366
  27.5 1.1 mix.1
  28.6 5.0 %all-to-all-start.1 = ((bf16[32,32,256]{2,1,0:T(8,128)(2,1)}), bf16[32,32,256]{2,1,0:T(8,128)(2,1)S(1)}, u32[]{:S(2)}, u32[]{:S(2)}) async-start(bf16[32,32,256]{2,1,0:T(8,128)(2,1)} %get-tuple-element.17), calls=%async_computation.1 | async-start | bytes 1048576 | tf_op jit(solution)/shard_map/all_to_all | solution.py:369
  33.6 2.1 %dynamic-slice_bitcast_fusion = (bf16[16,64,256]{2,1,0:T(8,128)(2,1)}, bf16[16,64,256]{2,1,0:T(8,128)(2,1)S(1)}) fusion(bf16[2,16,64,256]{3,2,1,0:T(8,128)(2,1)} %bitcast.71, s32[]{:T(128)S(6)} %select_n.136, s32[]{:T(128)S(6)} %select_n.134), kind=kLoop, calls=%fused_computation.11 | loop fusion | bytes 2097160 | tf_op jit(solution)/shard_map/jit(dynamic_index_in_dim)/squeeze | solution.py:372
  35.7 0.1 pad_maximum_fusion.5
  35.8 0.1 copy.39.inv_ref
  35.9 0.2 copy.37
  36.2 2.1 %copy.38 = bf16[1024,256]{0,1:T(8,128)(2,1)} copy(bf16[1024,256]{1,0:T(8,128)(2,1)} %param.9) | data formatting | bytes 1048576 | tf_op args[4]
  38.2 0.1 fusion.34.invt_ref
  38.3 7.0 %all-to-all-done.1 = bf16[32,32,256]{2,1,0:T(8,128)(2,1)S(1)} async-done(((bf16[32,32,256]{2,1,0:T(8,128)(2,1)}), bf16[32,32,256]{2,1,0:T(8,128)(2,1)S(1)}, u32[]{:S(2)}, u32[]{:S(2)}) %all-to-all-start.1) | async-done | bytes 524320 | tf_op jit(solution)/shard_map/all_to_all | solution.py:369
  45.3 1.0 copy-done.2
  46.3 10.7 %mlp.1 = (bf16[2048,256]{1,0:T(8,128)(2,1)}, bf16[2048,1024]{1,0:T(8,128)(2,1)}, bf16[2048,1024]{1,0:T(8,128)(2,1)}, bf16[1024,256]{1,0:T(8,128)(2,1)}) custom-call(bf16[1024,256]{1,0:T(8,128)(2,1)S(1)} %bitcast.68, bf16[16,64,256]{2,1,0:T(8,128)(2,1)S(1)} %get-tuple-element.33.own_ref, bf16[16,64,256]{2,1,0:T(8,128)(2,1)} %collective-permute-done.3.par_ref, ...), custom_call_target="tpu_custom_call" | custom-call | tf_op jit(solution)/shard_map/mlp/pallas_call | solution.py:107
  57.0 5.0 %all-to-all-start.2 = ((bf16[32,32,256]{2,1,0:T(8,128)(2,1)}), bf16[32,32,256]{2,1,0:T(8,128)(2,1)S(1)}, u32[]{:S(2)}, u32[]{:S(2)}) async-start(bf16[32,32,256]{2,1,0:T(8,128)(2,1)} %bitcast.75), calls=%async_computation.2 | async-start | bytes 1048576 | tf_op jit(solution)/shard_map/all_to_all | solution.py:369
  62.0 7.2 %grads.1 = (f32[32,32,256]{2,1,0:T(8,128)S(1)}, bf16[32,32,256]{2,1,0:T(8,128)(2,1)}) custom-call(s32[1]{0:T(128)} %bitcast.2.core_ref, bf16[2048,256]{1,0:T(8,128)(2,1)} %get-tuple-element.21.hid_ref, bf16[2048,1024]{1,0:T(8,128)(2,1)} %get-tuple-element.22.dpre_ref, bf16[2048,1024]{1,0:T(8,128)(2,1)} %get-tuple-element.23.act_ref, ...), custom_call_target="tpu_custom_call" | custom-call | tf_op jit(solution)/shard_map/grads/pallas_call | solution.py:193
  69.2 0.5 collective-permute-start.1
  69.7 2.8 %all-to-all-done.2.recv_ref = bf16[32,32,256]{2,1,0:T(8,128)(2,1)S(1)} async-done(((bf16[32,32,256]{2,1,0:T(8,128)(2,1)}), bf16[32,32,256]{2,1,0:T(8,128)(2,1)S(1)}, u32[]{:S(2)}, u32[]{:S(2)}) %all-to-all-start.2) | async-done | bytes 524320 | tf_op jit(solution)/shard_map/all_to_all | solution.py:369
  72.6 0.1 sum_parts.3.d_ref
  72.7 0.1 collective-permute-start.4
  72.8 1.1 collective-permute-done.4.dpar_ref
  73.9 1.1 last.1
  75.1 18.4 %all_to_all.26.recv_ref = bf16[32,40,256]{2,1,0:T(8,128)(2,1)S(1)} all-to-all(bf16[32,40,256]{2,1,0:T(8,128)(2,1)S(1)} %get-tuple-element.26), channel_id=1, replica_groups={{0,2,4,6,8,10,12,14,16,18,20,22,24,26,28,30,32,34,36,38,40,42,44,46,48,..., dimensions={0} | all-to-all | bytes 1310720 | tf_op jit(solution)/shard_map/all_to_all | solution.py:369
  93.4 5.0 %all-to-all-start.4 = ((bf16[32,32,256]{2,1,0:T(8,128)(2,1)}), bf16[32,32,256]{2,1,0:T(8,128)(2,1)S(1)}, u32[]{:S(2)}, u32[]{:S(2)}) async-start(bf16[32,32,256]{2,1,0:T(8,128)(2,1)} %get-tuple-element.28), calls=%async_computation.4 | async-start | bytes 1048576 | tf_op jit(solution)/shard_map/all_to_all | solution.py:369
  98.5 0.1 lines_rows.1
  98.6 3.5 %collective-permute-start.7 = (bf16[72,256]{1,0:T(8,128)(2,1)S(1)}, bf16[72,256]{1,0:T(8,128)(2,1)S(1)}, u32[]{:S(2)}, u32[]{:S(2)}) collective-permute-start(bf16[72,256]{1,0:T(8,128)(2,1)S(1)} %get-tuple-element.34), channel_id=1, source_target_pairs={{0,64},{64,128},{128,192},{192,0},{1,65},{65,129},{129,193},{193,1... | collective-permute-start | bytes 110600 | tf_op jit(solution)/shard_map/ppermute | solution.py:413
  102.1 4.5 %collective-permute-start.8 = (bf16[72,256]{1,0:T(8,128)(2,1)S(1)}, bf16[72,256]{1,0:T(8,128)(2,1)S(1)}, u32[]{:S(2)}, u32[]{:S(2)}) collective-permute-start(bf16[72,256]{1,0:T(8,128)(2,1)S(1)} %get-tuple-element.36), channel_id=1, source_target_pairs={{0,128},{64,192},{128,0},{192,64},{1,129},{65,193},{129,1},{193,65... | collective-permute-start | bytes 110600 | tf_op jit(solution)/shard_map/ppermute | solution.py:413
  106.6 2.7 %collective-permute-start.9 = (bf16[72,256]{1,0:T(8,128)(2,1)S(1)}, bf16[72,256]{1,0:T(8,128)(2,1)S(1)}, u32[]{:S(2)}, u32[]{:S(2)}) collective-permute-start(bf16[72,256]{1,0:T(8,128)(2,1)S(1)} %get-tuple-element.35), channel_id=1, source_target_pairs={{0,192},{64,0},{128,64},{192,128},{1,193},{65,1},{129,65},{193,129... | collective-permute-start | bytes 110600 | tf_op jit(solution)/shard_map/ppermute | solution.py:413
  109.3 1.9 %collective-permute-done.7 = bf16[72,256]{1,0:T(8,128)(2,1)S(1)} collective-permute-done((bf16[72,256]{1,0:T(8,128)(2,1)S(1)}, bf16[72,256]{1,0:T(8,128)(2,1)S(1)}, u32[]{:S(2)}, u32[]{:S(2)}) %collective-permute-start.7) | collective-permute-done | bytes 36896 | tf_op jit(solution)/shard_map/ppermute | solution.py:413
  111.2 1.7 %collective-permute-done.8 = bf16[72,256]{1,0:T(8,128)(2,1)S(1)} collective-permute-done((bf16[72,256]{1,0:T(8,128)(2,1)S(1)}, bf16[72,256]{1,0:T(8,128)(2,1)S(1)}, u32[]{:S(2)}, u32[]{:S(2)}) %collective-permute-start.8) | collective-permute-done | bytes 36896 | tf_op jit(solution)/shard_map/ppermute | solution.py:413
  113.0 0.1 collective-permute-start.6
  113.1 0.5 collective-permute-start.10
  113.6 0.6 copy.54
  114.2 0.7 collective-permute-done.10
  115.0 0.6 fusion.27
  115.7 0.3 convolution_bitcast_fusion.1
  116.0 0.3 convolution_bitcast_fusion
  116.4 0.5 copy-done.5
  116.9 1.4 %fusion = bf16[32,64,256]{2,1,0:T(8,128)(2,1)} fusion(f32[16,64,256]{2,1,0:T(8,128)S(1)} %convolution_bitcast_fusion, f32[16,64,256]{2,1,0:T(8,128)S(1)} %convolution_bitcast_fusion.1, bf16[32,64,256]{2,1,0:T(8,128)(2,1)S(1)} %copy-done.5), kind=kLoop, calls=%fused_computation.1 | loop fusion | flops 2097152 | bytes 4194304 | tf_op jit(solution)/shard_map/convert_element_type | solution.py:428
  (43 shorter events, 0.5 us)
Async XLA Ops:
  0.6 1.2 %copy-start = (bf16[32,64,256]{2,1,0:T(8,128)(2,1)S(1)}, bf16[32,64,256]{2,1,0:T(8,128)(2,1)}, u32[]{:S(2)}) copy-start(bf16[32,64,256]{2,1,0:T(8,128)(2,1)} %param.5) | copy-start | bytes 3145732
  1.9 2.0 %collective-permute-start = (bf16[16,64,256]{2,1,0:T(8,128)(2,1)S(1)}, bf16[16,64,256]{2,1,0:T(8,128)(2,1)S(1)}, u32[]{:S(2)}, u32[]{:S(2)}) collective-permute-start(bf16[16,64,256]{2,1,0:T(8,128)(2,1)S(1)} %dynamic-slice_bitcast_fusion.2), channel_id=1, source_target_pairs={{0,1},{1,0},{2,3},{3,2},{4,5},{5,4},{6,7},{7,6},{8,9},{9,8},{10,11... | collective-permute-start | bytes 1572872 | tf_op jit(solution)/shard_map/ppermute | solution.py:366
  2.2 2.0 %copy-start.6 = (bf16[64,32,2]{0,2,1:T(2,128)(2,1)}, bf16[64,32,2]{0,2,1:T(2,128)(2,1)S(1)}, u32[]{:S(2)}) copy-start(bf16[64,32,2]{0,2,1:T(2,128)(2,1)S(1)} %copy.31) | copy-start | bytes 24580
  26.1 9.9 %copy-start.1 = (bf16[256,1024]{1,0:T(8,128)(2,1)S(1)}, bf16[256,1024]{1,0:T(8,128)(2,1)}, u32[]{:S(2)}) copy-start(bf16[256,1024]{1,0:T(8,128)(2,1)} %wi_ref.1) | copy-start | bytes 1572868
  26.1 1.4 %collective-permute-start.2 = (bf16[32,8,256]{2,1,0:T(8,128)(2,1)S(1)}, bf16[32,8,256]{2,1,0:T(8,128)(2,1)S(1)}, u32[]{:S(2)}, u32[]{:S(2)}) collective-permute-start(bf16[32,8,256]{2,1,0:T(8,128)(2,1)S(1)} %slice.12.own_ref), channel_id=1, source_target_pairs={{0,1},{1,0},{2,3},{3,2},{4,5},{5,4},{6,7},{7,6},{8,9},{9,8},{10,11... | collective-permute-start | bytes 393224 | tf_op jit(solution)/shard_map/ppermute | solution.py:366
  28.6 16.7 %all-to-all-start.1 = ((bf16[32,32,256]{2,1,0:T(8,128)(2,1)}), bf16[32,32,256]{2,1,0:T(8,128)(2,1)S(1)}, u32[]{:S(2)}, u32[]{:S(2)}) async-start(bf16[32,32,256]{2,1,0:T(8,128)(2,1)} %get-tuple-element.17), calls=%async_computation.1 | async-start | bytes 1048576 | tf_op jit(solution)/shard_map/all_to_all | solution.py:369
  35.7 2.6 %collective-permute-start.3 = (bf16[16,64,256]{2,1,0:T(8,128)(2,1)}, bf16[16,64,256]{2,1,0:T(8,128)(2,1)}, u32[]{:S(2)}, u32[]{:S(2)}) collective-permute-start(bf16[16,64,256]{2,1,0:T(8,128)(2,1)} %get-tuple-element.32), channel_id=1, source_target_pairs={{0,1},{1,0},{2,3},{3,2},{4,5},{5,4},{6,7},{7,6},{8,9},{9,8},{10,11... | collective-permute-start | bytes 1572872 | tf_op jit(solution)/shard_map/ppermute | solution.py:366
  45.3 1.0 copy-start.2
  57.0 15.6 %all-to-all-start.2 = ((bf16[32,32,256]{2,1,0:T(8,128)(2,1)}), bf16[32,32,256]{2,1,0:T(8,128)(2,1)S(1)}, u32[]{:S(2)}, u32[]{:S(2)}) async-start(bf16[32,32,256]{2,1,0:T(8,128)(2,1)} %bitcast.75), calls=%async_computation.2 | async-start | bytes 1048576 | tf_op jit(solution)/shard_map/all_to_all | solution.py:369
  62.0 11.9 %copy-start.3 = (bf16[256,256]{1,0:T(8,128)(2,1)S(1)}, bf16[256,256]{1,0:T(8,128)(2,1)}, u32[]{:S(2)}) copy-start(bf16[256,256]{1,0:T(8,128)(2,1)} %get-tuple-element.19.re_ref) | copy-start | bytes 393220
  62.0 11.9 %copy-start.4 = (bf16[256,256]{1,0:T(8,128)(2,1)S(1)}, bf16[256,256]{1,0:T(8,128)(2,1)}, u32[]{:S(2)}) copy-start(bf16[256,256]{1,0:T(8,128)(2,1)} %get-tuple-element.20.im_ref) | copy-start | bytes 393220
  69.2 3.5 %collective-permute-start.5 = (bf16[32,32,256]{2,1,0:T(8,128)(2,1)}, bf16[32,32,256]{2,1,0:T(8,128)(2,1)S(1)}, u32[]{:S(2)}, u32[]{:S(2)}) collective-permute-start(bf16[32,32,256]{2,1,0:T(8,128)(2,1)} %get-tuple-element.25), channel_id=1, source_target_pairs={{0,1},{1,0},{2,3},{3,2},{4,5},{5,4},{6,7},{7,6},{8,9},{9,8},{10,11... | collective-permute-start | bytes 1572872 | tf_op jit(solution)/shard_map/ppermute | solution.py:366
  69.2 3.5 %collective-permute-start.1 = (bf16[32,256]{1,0:T(8,128)(2,1)S(1)}, bf16[32,256]{1,0:T(8,128)(2,1)S(1)}, u32[]{:S(2)}, u32[]{:S(2)}) collective-permute-start(bf16[32,256]{1,0:T(8,128)(2,1)S(1)} %sum_parts.2.u_ref), channel_id=1, source_target_pairs={{0,1},{1,0},{2,3},{3,2},{4,5},{5,4},{6,7},{7,6},{8,9},{9,8},{10,11... | collective-permute-start | bytes 49160 | tf_op jit(solution)/shard_map/ppermute | solution.py:366
  72.7 1.3 %collective-permute-start.4 = (bf16[32,256]{1,0:T(8,128)(2,1)S(1)}, bf16[32,256]{1,0:T(8,128)(2,1)S(1)}, u32[]{:S(2)}, u32[]{:S(2)}) collective-permute-start(bf16[32,256]{1,0:T(8,128)(2,1)S(1)} %sum_parts.3.d_ref), channel_id=1, source_target_pairs={{0,1},{1,0},{2,3},{3,2},{4,5},{5,4},{6,7},{7,6},{8,9},{9,8},{10,11... | collective-permute-start | bytes 49160 | tf_op jit(solution)/shard_map/ppermute | solution.py:366
  93.4 19.5 %all-to-all-start.4 = ((bf16[32,32,256]{2,1,0:T(8,128)(2,1)}), bf16[32,32,256]{2,1,0:T(8,128)(2,1)S(1)}, u32[]{:S(2)}, u32[]{:S(2)}) async-start(bf16[32,32,256]{2,1,0:T(8,128)(2,1)} %get-tuple-element.28), calls=%async_computation.4 | async-start | bytes 1048576 | tf_op jit(solution)/shard_map/all_to_all | solution.py:369
  98.4 17.2 %copy-start.7 = (bf16[64,32,2]{0,2,1:T(2,128)(2,1)S(1)}, bf16[64,32,2]{0,2,1:T(2,128)(2,1)}, u32[]{:S(2)}) copy-start(bf16[64,32,2]{0,2,1:T(2,128)(2,1)} %copy-done.6) | copy-start | bytes 24580
  98.6 12.6 %collective-permute-start.7 = (bf16[72,256]{1,0:T(8,128)(2,1)S(1)}, bf16[72,256]{1,0:T(8,128)(2,1)S(1)}, u32[]{:S(2)}, u32[]{:S(2)}) collective-permute-start(bf16[72,256]{1,0:T(8,128)(2,1)S(1)} %get-tuple-element.34), channel_id=1, source_target_pairs={{0,64},{64,128},{128,192},{192,0},{1,65},{65,129},{129,193},{193,1... | collective-permute-start | bytes 110600 | tf_op jit(solution)/shard_map/ppermute | solution.py:413
  102.1 10.8 %collective-permute-start.8 = (bf16[72,256]{1,0:T(8,128)(2,1)S(1)}, bf16[72,256]{1,0:T(8,128)(2,1)S(1)}, u32[]{:S(2)}, u32[]{:S(2)}) collective-permute-start(bf16[72,256]{1,0:T(8,128)(2,1)S(1)} %get-tuple-element.36), channel_id=1, source_target_pairs={{0,128},{64,192},{128,0},{192,64},{1,129},{65,193},{129,1},{193,65... | collective-permute-start | bytes 110600 | tf_op jit(solution)/shard_map/ppermute | solution.py:413
  106.6 6.3 %collective-permute-start.9 = (bf16[72,256]{1,0:T(8,128)(2,1)S(1)}, bf16[72,256]{1,0:T(8,128)(2,1)S(1)}, u32[]{:S(2)}, u32[]{:S(2)}) collective-permute-start(bf16[72,256]{1,0:T(8,128)(2,1)S(1)} %get-tuple-element.35), channel_id=1, source_target_pairs={{0,192},{64,0},{128,64},{192,128},{1,193},{65,1},{129,65},{193,129... | collective-permute-start | bytes 110600 | tf_op jit(solution)/shard_map/ppermute | solution.py:413
  113.0 2.6 %collective-permute-start.6 = (bf16[32,32,256]{2,1,0:T(8,128)(2,1)S(1)}, bf16[32,32,256]{2,1,0:T(8,128)(2,1)S(1)}, u32[]{:S(2)}, u32[]{:S(2)}) collective-permute-start(bf16[32,32,256]{2,1,0:T(8,128)(2,1)S(1)} %all-to-all-done.4), channel_id=1, source_target_pairs={{0,1},{1,0},{2,3},{3,2},{4,5},{5,4},{6,7},{7,6},{8,9},{9,8},{10,11... | collective-permute-start | bytes 1572872 | tf_op jit(solution)/shard_map/ppermute | solution.py:366
  113.1 1.9 %collective-permute-start.10 = (f32[4,256]{1,0:T(4,128)S(1)}, f32[4,256]{1,0:T(4,128)S(1)}, u32[]{:S(2)}, u32[]{:S(2)}) collective-permute-start(f32[4,256]{1,0:T(4,128)S(1)} %dynamic-slice_bitcast_fusion.6), channel_id=1, source_target_pairs={{0,1},{1,0},{2,3},{3,2},{4,5},{5,4},{6,7},{7,6},{8,9},{9,8},{10,11... | collective-permute-start | bytes 12296 | tf_op jit(solution)/shard_map/ppermute | solution.py:366
  115.7 1.2 %copy-start.5 = (bf16[32,64,256]{2,1,0:T(8,128)(2,1)S(1)}, bf16[32,64,256]{2,1,0:T(8,128)(2,1)}, u32[]{:S(2)}) copy-start(bf16[32,64,256]{2,1,0:T(8,128)(2,1)} %param.6) | copy-start | bytes 3145732

commit v4 on v3

--- a/solution.py
+++ b/solution.py
@@ -1,3 +1,4 @@
+import functools
 import math
 
 import jax
@@ -137,10 +138,15 @@
     )(mix, own, par, inv, inv.T, w_in, w_in.T, w_out_t)
 
 
+def by_half(low, high):
+    row = lax.broadcasted_iota(jnp.int32, low.shape, 1)
+    return jnp.where(row < 4, low, high)
+
+
 def grads_kernel(core_ref, hid_ref, dpre_ref, act_ref, own_ref, par_ref, keep_ref, send_ref, acc_in, acc_out):
     i = pl.program_id(0)
-    block, cols, _ = own_ref.shape
-    chips, kept, _ = keep_ref.shape
+    block, cols, chan = own_ref.shape
+    chips, kept, chan = keep_ref.shape
     groups = kept // 8
 
     @pl.when(i == 0)
@@ -153,29 +159,18 @@
     cot = jnp.concatenate([own_ref[...].reshape(flat), par_ref[...].reshape(flat)], axis=0)
     acc_out[...] += rows_dot(cot, act_ref[...])
 
-    def store(ref, acc):
-        full = acc[...].T
+    @pl.when(i == pl.num_programs(0) - 1)
+    def _():
+        even = core_ref[0] == 0
+        g_in = acc_in[...].T.reshape(groups * chips, 8, chan)
+        g_out = acc_out[...].T.reshape(groups * chips, 8, chan)
+        lows = by_half(g_in, pltpu.roll(g_out, 4, 1))
+        highs = by_half(pltpu.roll(g_in, 4, 1), g_out)
+        keep = jnp.where(even, lows, highs)
+        send = jnp.where(even, highs, lows)
         for t in range(chips):
-            for g in range(groups):
-                top = (g * chips + t) * 8
-                if ref.dtype == F32:
-                    ref[t, g * 8 : (g + 1) * 8, :] = full[top : top + 8]
-            if ref.dtype != F32:
-                ref[t] = jnp.concatenate(
-                    [full[(g * chips + t) * 8 : (g * chips + t) * 8 + 8] for g in range(groups)], axis=0
-                ).astype(ref.dtype)
-
-    last = i == pl.num_programs(0) - 1
-
-    @pl.when(last & (core_ref[0] == 0))
-    def _():
-        store(keep_ref, acc_in)
-        store(send_ref, acc_out)
-
-    @pl.when(last & (core_ref[0] != 0))
-    def _():
-        store(keep_ref, acc_out)
-        store(send_ref, acc_in)
+            keep_ref[t] = jnp.concatenate([keep[g * chips + t] for g in range(groups)], axis=0)
+            send_ref[t] = jnp.concatenate([send[g * chips + t] for g in range(groups)], axis=0).astype(BF)
 
 
 def in_hbm(x):
@@ -235,11 +230,6 @@
         compiler_params=pltpu.CompilerParams(vmem_limit_bytes=6 << 20),
         name="sum_parts",
     )(recv)
-
-
-def by_half(low, high):
-    row = lax.broadcasted_iota(jnp.int32, low.shape, 1)
-    return jnp.where(row < 4, low, high)
 
 
 def mix_kernel(core_ref, u_ref, own_ref, par_ref, out_ref, re_ref, im_ref):
@@ -348,6 +338,54 @@
     )(recv)
 
 
+def final_kernel(own_ref, one_ref, two_ref, three_ref, mode_ref, in_ref, out_ref, *, scale_mlp, scale_mode):
+    total = own_ref[...].astype(F32)
+    for ref in (one_ref, two_ref, three_ref):
+        total = total + ref[...].astype(F32)
+    in_ref[...] = total[:4] * scale_mlp
+    out_ref[...] = total[4:8] * scale_mlp
+    for k in range(mode_ref.shape[1]):
+        mode_ref[0, k] = total[8 * k + 8 : 8 * k + 12] * scale_mode
+        mode_ref[1, k] = total[8 * k + 12 : 8 * k + 16] * scale_mode
+
+
+def final_call(parts, scale_mlp, scale_mode):
+    rows, chan = parts[0].shape
+    vmem = pl.BlockSpec(memory_space=pltpu.VMEM)
+    return pl.pallas_call(
+        functools.partial(final_kernel, scale_mlp=scale_mlp, scale_mode=scale_mode),
+        in_specs=[vmem] * 4,
+        out_specs=[vmem] * 3,
+        out_shape=[
+            jax.ShapeDtypeStruct((2, rows // 8 - 1, 4, chan), F32),
+            jax.ShapeDtypeStruct((4, chan), F32),
+            jax.ShapeDtypeStruct((4, chan), F32),
+        ],
+        compiler_params=pltpu.CompilerParams(vmem_limit_bytes=4 << 20),
+        name="final",
+    )(*parts)
+
+
+def own_kernel(gy_ref, blocks_ref, out_ref):
+    out_ref[...] = blocks_ref[0]
+
+
+def own_call(gy, blocks):
+    _, rows, chan = blocks.shape
+    return pl.pallas_call(
+        own_kernel,
+        grid_spec=pltpu.PrefetchScalarGridSpec(
+            num_scalar_prefetch=1,
+            grid=(1,),
+            in_specs=[pl.BlockSpec((1, rows, chan), lambda i, g: (g[0], 0, 0))],
+            out_specs=pl.BlockSpec((rows, chan), lambda i, g: (0, 0)),
+        ),
+        out_shape=jax.ShapeDtypeStruct((rows, chan), BF),
+        compiler_params=pltpu.CompilerParams(vmem_limit_bytes=2 << 20),
+        name="own_rows",
+    )(gy.reshape(1), blocks)
+
+
 def local(inputs, cotangent, mode_weight, w_in, w_out):
     lines, cols, chan = inputs.shape
     nx = lax.axis_size("gx")
@@ -394,7 +432,7 @@
     mixed = spread(sent)
     spec_par = pair(spec)
     hidden, act, d_pre, d_part = mlp_call(
-        mixed.reshape(2 * M * half, chan), cot_own, cot_par, inv, w_in, w_out.T
+        mixed.reshape(2 * M * half, chan), cot_own, cot_par, inv, w_in, in_hbm(w_out.T)
     )
     dv = spread(d_part.reshape(chips, both, chan))
     g_own, g_send = grads_call(core, hidden, d_pre, act, cot_own, cot_par, chips)
@@ -407,18 +445,13 @@
     du_own = spread(du)
     du_par = pair(du_own)
     blocks = lines_call(recv, ny)
-    total = pick(blocks, gy, 0).astype(F32)
+    scale_mlp = 1.0 / math.sqrt(lines * ny * total_x)
+    scale_mode = 1.0 / math.sqrt(lines * ny)
+    parts = [own_call(gy, blocks)]
     for d in range(1, ny):
         sent = pick(blocks, (gy + d) % ny, 0)
-        moved = lax.ppermute(sent, "gy", [(i, (i + d) % ny) for i in range(ny)])
-        total = total + moved.astype(F32)
-    mine, other = total[: 2 * own_rows], total[2 * own_rows :]
-    mine = mine.reshape(2, own_rows, chan)
-    swapped = pair(pick(mine, 1 - core, 0))
-    mine = pick(mine, core, 0)
-    tail_in = jnp.where(core == 0, mine, swapped)
-    tail_out = jnp.where(core == 0, swapped, mine)
-    d_mode = other.reshape(M // ny, 2, own_rows, chan).transpose(1, 0, 2, 3)
+        parts.append(lax.ppermute(sent, "gy", [(i, (i + d) % ny) for i in range(ny)]))
+    d_mode, tail_in, tail_out = final_call(parts, scale_mlp, scale_mode)
 
     du_lo = jnp.where(core == 0, du_own, du_par).reshape(2 * M, half, chan)
     du_hi = jnp.where(core == 0, du_par, du_own).reshape(2 * M, half, chan)
@@ -426,9 +459,7 @@
     ret_hi = contract("myc,xm->yxc", du_hi, own_fwd)
     returned = jnp.concatenate([ret_lo, ret_hi], axis=0)
     d_inputs = (cotangent.astype(F32) + returned).astype(BF)
-    scale_mlp = 1.0 / math.sqrt(lines * ny * total_x)
-    scale_mode = 1.0 / math.sqrt(lines * ny)
-    return (d_inputs, d_mode * scale_mode, tail_in.T * scale_mlp, tail_out * scale_mlp)
+    return (d_inputs, d_mode, tail_in.T, tail_out)
 
 
 def solution(mesh):

time: 120 us -> 125 us (1.042)
  blocking collectives: 39.8 us -> 54.6 us
  starting transfers between devices: 27.1 us -> 21.3 us
  waiting for transfers between devices: 16.9 us -> 15 us
  local copies, waits for them, and re-layouts: 9.36 us -> 7.63 us
    all_to_all x2 -> x3, blocking collectives: 39.8 us -> 54.6 us  [spread(): return lax.all_to_all(x, 'gx', 0, 0, tiled=True, axis_index_groups=groups)]
    all_to_all x3 -> x2, starting transfers between devices: 15 us -> 10 us  [spread(): return lax.all_to_all(x, 'gx', 0, 0, tiled=True, axis_index_groups=groups)]
    unnamed x18 -> x12, local copies, waits for them, and re-layouts: 5.07 us -> 4.01 us
    ppermute x8 -> x7, waiting for transfers between devices: 3.47 us -> 2.74 us  [pair(): return lax.ppermute(x, 'gx', swap)]
    all_to_all x3 -> x2, waiting for transfers between devices: 9.82 us -> 9.7 us  [spread(): return lax.all_to_all(x, 'gx', 0, 0, tiled=True, axis_index_groups=groups)]
  transfers between devices with their start and end apart: 14 -> 12, of which waited for: 8 -> 7; matrix products, arithmetic and copies ran while one was open for 6% -> 5% of each run, Pallas kernels for 6% -> 7%
where the time goes in v4:
time: 125 us; the launch traced here: 123 us
  blocking collectives  54.6 us (44%)
  starting transfers between devices  21.3 us (17%)
  Pallas kernels  20.6 us (16%)
  waiting for transfers between devices  15 us (12%)
  local copies, waits for them, and re-layouts  7.63 us (6%)
  other arithmetic  1.83 us (1%)
    all_to_all x3, blocking collectives, spread(): return lax.all_to_all(x, 'gx', 0, 0, tiled=True, axis_index_groups=groups)  54.6 us
    pallas_call x1, Pallas kernels, mlp_call(): pl.pallas_call(mlp_kernel, grid=(half // block,), in_specs=[pl.BlockSpec(...  10.9 us
    ppermute x3, starting transfers between devices, local(): lax.ppermute(sent, 'gy', [(i, (i + d) % ny) for i in range(ny)])  10.5 us
    all_to_all x2, starting transfers between devices, spread(): return lax.all_to_all(x, 'gx', 0, 0, tiled=True, axis_index_groups=groups)  10 us
    all_to_all x2, waiting for transfers between devices, spread(): return lax.all_to_all(x, 'gx', 0, 0, tiled=True, axis_index_groups=groups)  9.7 us
    pallas_call x1, Pallas kernels, grads_call(): pl.pallas_call(grads_kernel, grid_spec=pltpu.PrefetchScalarGridSpec(num_s...  7.31 us
    unnamed x12, local copies, waits for them, and re-layouts  4.01 us
    ppermute x7, waiting for transfers between devices, pair(): return lax.ppermute(x, 'gx', swap)  2.74 us
  transfers between devices with their start and end apart: 12, of which 7 were waited for; matrix products, arithmetic and copies ran while one was open for 5% of the time, Pallas kernels for 7%

profile of v4, /device:TPU:2, one launch (start us, length us, event | category | flops | bytes accessed | tf_op | source)
XLA Modules:
  0.0 123.2 jit_solution(7125106895622801494)
XLA Ops:
  0.6 0.0 copy-start
  0.7 1.2 copy-done
  1.9 0.1 collective-permute-start
  2.0 0.2 multiply_convert_fusion.3
  2.3 1.0 copy.32
  3.3 0.3 fusion.2
  3.6 0.3 collective-permute-done
  3.9 0.3 fusion.1
  4.2 0.3 copy.31
  4.6 21.5 %all_to_all.25.recv_ref = bf16[32,40,256]{2,1,0:T(8,128)(2,1)S(1)} all-to-all(bf16[32,40,256]{2,1,0:T(8,128)(2,1)S(1)} %pad_maximum_fusion), channel_id=1, replica_groups={{0,2,4,6,8,10,12,14,16,18,20,22,24,26,28,30,32,34,36,38,40,42,44,46,48,..., dimensions={0} | all-to-all | bytes 1310720 | tf_op jit(solution)/shard_map/all_to_all | solution.py:407
  26.1 0.0 copy-start.1
  26.1 0.1 collective-permute-start.2
  26.2 0.1 sum_parts.2.u_ref
  26.3 1.3 %collective-permute-done.2.par_ref = bf16[32,8,256]{2,1,0:T(8,128)(2,1)S(1)} collective-permute-done((bf16[32,8,256]{2,1,0:T(8,128)(2,1)S(1)}, bf16[32,8,256]{2,1,0:T(8,128)(2,1)S(1)}, u32[]{:S(2)}, u32[]{:S(2)}) %collective-permute-start.2) | collective-permute-done | bytes 131104 | tf_op jit(solution)/shard_map/ppermute | solution.py:404
  27.5 1.1 mix.1
  28.6 5.0 %all-to-all-start.1 = ((bf16[32,32,256]{2,1,0:T(8,128)(2,1)}), bf16[32,32,256]{2,1,0:T(8,128)(2,1)S(1)}, u32[]{:S(2)}, u32[]{:S(2)}) async-start(bf16[32,32,256]{2,1,0:T(8,128)(2,1)} %get-tuple-element.20), calls=%async_computation.1 | async-start | bytes 1048576 | tf_op jit(solution)/shard_map/all_to_all | solution.py:407
  33.6 2.1 %dynamic-slice_bitcast_fusion = (bf16[16,64,256]{2,1,0:T(8,128)(2,1)}, bf16[16,64,256]{2,1,0:T(8,128)(2,1)S(1)}) fusion(bf16[2,16,64,256]{3,2,1,0:T(8,128)(2,1)} %bitcast.53, s32[]{:T(128)S(6)} %select_n.118, s32[]{:T(128)S(6)} %select_n.116), kind=kLoop, calls=%fused_computation.11 | loop fusion | bytes 2097160 | tf_op jit(solution)/shard_map/jit(dynamic_index_in_dim)/squeeze | solution.py:410
  35.8 0.1 pad_maximum_fusion.5
  35.8 0.1 copy.37.inv_ref
  36.0 0.2 copy.35
  36.2 2.0 %copy.36 = bf16[1024,256]{0,1:T(8,128)(2,1)} copy(bf16[1024,256]{1,0:T(8,128)(2,1)} %param.9) | data formatting | bytes 1048576 | tf_op args[4]
  38.2 0.1 fusion.29.invt_ref
  38.3 7.0 %all-to-all-done.1 = bf16[32,32,256]{2,1,0:T(8,128)(2,1)S(1)} async-done(((bf16[32,32,256]{2,1,0:T(8,128)(2,1)}), bf16[32,32,256]{2,1,0:T(8,128)(2,1)S(1)}, u32[]{:S(2)}, u32[]{:S(2)}) %all-to-all-start.1) | async-done | bytes 524320 | tf_op jit(solution)/shard_map/all_to_all | solution.py:407
  45.3 10.9 %mlp.1 = (bf16[2048,256]{1,0:T(8,128)(2,1)}, bf16[2048,1024]{1,0:T(8,128)(2,1)}, bf16[2048,1024]{1,0:T(8,128)(2,1)}, bf16[1024,256]{1,0:T(8,128)(2,1)}) custom-call(bf16[1024,256]{1,0:T(8,128)(2,1)S(1)} %bitcast.51, bf16[16,64,256]{2,1,0:T(8,128)(2,1)S(1)} %get-tuple-element.39.own_ref, bf16[16,64,256]{2,1,0:T(8,128)(2,1)} %collective-permute-done.3.par_ref, ...), custom_call_target="tpu_custom_call" | custom-call | tf_op jit(solution)/shard_map/mlp/pallas_call | solution.py:108
  56.2 5.0 %all-to-all-start.2 = ((bf16[32,32,256]{2,1,0:T(8,128)(2,1)}), bf16[32,32,256]{2,1,0:T(8,128)(2,1)S(1)}, u32[]{:S(2)}, u32[]{:S(2)}) async-start(bf16[32,32,256]{2,1,0:T(8,128)(2,1)} %bitcast.58), calls=%async_computation.2 | async-start | bytes 1048576 | tf_op jit(solution)/shard_map/all_to_all | solution.py:407
  61.3 7.3 %grads.1 = (f32[32,32,256]{2,1,0:T(8,128)S(1)}, bf16[32,32,256]{2,1,0:T(8,128)(2,1)}) custom-call(s32[1]{0:T(128)} %bitcast.2.core_ref, bf16[2048,256]{1,0:T(8,128)(2,1)} %get-tuple-element.24.hid_ref, bf16[2048,1024]{1,0:T(8,128)(2,1)} %get-tuple-element.25.dpre_ref, bf16[2048,1024]{1,0:T(8,128)(2,1)} %get-tuple-element.26.act_ref, ...), custom_call_target="tpu_custom_call" | custom-call | tf_op jit(solution)/shard_map/grads/pallas_call | solution.py:188
  68.6 0.5 collective-permute-start.1
  69.1 2.7 %all-to-all-done.2.recv_ref = bf16[32,32,256]{2,1,0:T(8,128)(2,1)S(1)} async-done(((bf16[32,32,256]{2,1,0:T(8,128)(2,1)}), bf16[32,32,256]{2,1,0:T(8,128)(2,1)S(1)}, u32[]{:S(2)}, u32[]{:S(2)}) %all-to-all-start.2) | async-done | bytes 524320 | tf_op jit(solution)/shard_map/all_to_all | solution.py:407
  71.8 0.1 sum_parts.3.d_ref
  71.9 0.1 collective-permute-start.4
  72.0 1.1 collective-permute-done.4.dpar_ref
  73.2 0.4 last.1
  73.6 18.5 %all_to_all.26.recv_ref = bf16[32,40,256]{2,1,0:T(8,128)(2,1)S(1)} all-to-all(bf16[32,40,256]{2,1,0:T(8,128)(2,1)S(1)} %get-tuple-element.29), channel_id=1, replica_groups={{0,2,4,6,8,10,12,14,16,18,20,22,24,26,28,30,32,34,36,38,40,42,44,46,48,..., dimensions={0} | all-to-all | bytes 1310720 | tf_op jit(solution)/shard_map/all_to_all | solution.py:407
  92.1 14.6 %all_to_all.27 = bf16[32,32,256]{2,1,0:T(8,128)(2,1)S(1)} all-to-all(bf16[32,32,256]{2,1,0:T(8,128)(2,1)S(1)} %get-tuple-element.31), channel_id=1, replica_groups={{0,2,4,6,8,10,12,14,16,18,20,22,24,26,28,30,32,34,36,38,40,42,44,46,48,..., dimensions={0} | all-to-all | bytes 1048576 | tf_op jit(solution)/shard_map/all_to_all | solution.py:407
  106.7 0.0 collective-permute-start.6
  106.7 0.1 lines_rows.1.blocks_ref
  106.8 3.3 %collective-permute-start.7 = (bf16[72,256]{1,0:T(8,128)(2,1)S(1)}, bf16[72,256]{1,0:T(8,128)(2,1)S(1)}, u32[]{:S(2)}, u32[]{:S(2)}) collective-permute-start(bf16[72,256]{1,0:T(8,128)(2,1)S(1)} %get-tuple-element.42), channel_id=1, source_target_pairs={{0,64},{64,128},{128,192},{192,0},{1,65},{65,129},{129,193},{193,1... | collective-permute-start | bytes 110600 | tf_op jit(solution)/shard_map/ppermute | solution.py:453
  110.1 4.5 %collective-permute-start.8 = (bf16[72,256]{1,0:T(8,128)(2,1)S(1)}, bf16[72,256]{1,0:T(8,128)(2,1)S(1)}, u32[]{:S(2)}, u32[]{:S(2)}) collective-permute-start(bf16[72,256]{1,0:T(8,128)(2,1)S(1)} %get-tuple-element.41), channel_id=1, source_target_pairs={{0,128},{64,192},{128,0},{192,64},{1,129},{65,193},{129,1},{193,65... | collective-permute-start | bytes 110600 | tf_op jit(solution)/shard_map/ppermute | solution.py:453
  114.6 2.7 %collective-permute-start.9 = (bf16[72,256]{1,0:T(8,128)(2,1)S(1)}, bf16[72,256]{1,0:T(8,128)(2,1)S(1)}, u32[]{:S(2)}, u32[]{:S(2)}) collective-permute-start(bf16[72,256]{1,0:T(8,128)(2,1)S(1)} %get-tuple-element.40), channel_id=1, source_target_pairs={{0,192},{64,0},{128,64},{192,128},{1,193},{65,1},{129,65},{193,129... | collective-permute-start | bytes 110600 | tf_op jit(solution)/shard_map/ppermute | solution.py:453
  117.3 1.2 collective-permute-done.8.two_ref
  118.5 1.4 %collective-permute-done.9.three_ref = bf16[72,256]{1,0:T(8,128)(2,1)S(1)} collective-permute-done((bf16[72,256]{1,0:T(8,128)(2,1)S(1)}, bf16[72,256]{1,0:T(8,128)(2,1)S(1)}, u32[]{:S(2)}, u32[]{:S(2)}) %collective-permute-start.9) | collective-permute-done | bytes 36896 | tf_op jit(solution)/shard_map/ppermute | solution.py:453
  119.9 0.7 final.1
  120.5 0.1 broadcast_select_fusion.1
  120.6 0.0 copy-start.4
  120.6 0.3 convolution_bitcast_fusion.1
  121.0 0.3 convolution_bitcast_fusion
  121.3 0.5 copy-done.4
  121.8 1.4 %fusion = bf16[32,64,256]{2,1,0:T(8,128)(2,1)} fusion(f32[16,64,256]{2,1,0:T(8,128)S(1)} %convolution_bitcast_fusion, f32[16,64,256]{2,1,0:T(8,128)S(1)} %convolution_bitcast_fusion.1, bf16[32,64,256]{2,1,0:T(8,128)(2,1)S(1)} %copy-done.4), kind=kLoop, calls=%fused_computation.1 | loop fusion | flops 2097152 | bytes 4194304 | tf_op jit(solution)/shard_map/convert_element_type | solution.py:461
  (28 shorter events, 0.3 us)
Async XLA Ops:
  0.6 1.2 copy-start
  1.9 2.0 %collective-permute-start = (bf16[16,64,256]{2,1,0:T(8,128)(2,1)S(1)}, bf16[16,64,256]{2,1,0:T(8,128)(2,1)S(1)}, u32[]{:S(2)}, u32[]{:S(2)}) collective-permute-start(bf16[16,64,256]{2,1,0:T(8,128)(2,1)S(1)} %dynamic-slice_bitcast_fusion.2), channel_id=1, source_target_pairs={{0,1},{1,0},{2,3},{3,2},{4,5},{5,4},{6,7},{7,6},{8,9},{9,8},{10,11... | collective-permute-start | bytes 1572872 | tf_op jit(solution)/shard_map/ppermute | solution.py:404
  26.1 9.9 %copy-start.1 = (bf16[256,1024]{1,0:T(8,128)(2,1)S(1)}, bf16[256,1024]{1,0:T(8,128)(2,1)}, u32[]{:S(2)}) copy-start(bf16[256,1024]{1,0:T(8,128)(2,1)} %wi_ref.1) | copy-start | bytes 1572868
  26.1 1.4 %collective-permute-start.2 = (bf16[32,8,256]{2,1,0:T(8,128)(2,1)S(1)}, bf16[32,8,256]{2,1,0:T(8,128)(2,1)S(1)}, u32[]{:S(2)}, u32[]{:S(2)}) collective-permute-start(bf16[32,8,256]{2,1,0:T(8,128)(2,1)S(1)} %slice.4.own_ref), channel_id=1, source_target_pairs={{0,1},{1,0},{2,3},{3,2},{4,5},{5,4},{6,7},{7,6},{8,9},{9,8},{10,11... | collective-permute-start | bytes 393224 | tf_op jit(solution)/shard_map/ppermute | solution.py:404
  28.6 16.7 %all-to-all-start.1 = ((bf16[32,32,256]{2,1,0:T(8,128)(2,1)}), bf16[32,32,256]{2,1,0:T(8,128)(2,1)S(1)}, u32[]{:S(2)}, u32[]{:S(2)}) async-start(bf16[32,32,256]{2,1,0:T(8,128)(2,1)} %get-tuple-element.20), calls=%async_computation.1 | async-start | bytes 1048576 | tf_op jit(solution)/shard_map/all_to_all | solution.py:407
  35.7 2.6 %collective-permute-start.3 = (bf16[16,64,256]{2,1,0:T(8,128)(2,1)}, bf16[16,64,256]{2,1,0:T(8,128)(2,1)}, u32[]{:S(2)}, u32[]{:S(2)}) collective-permute-start(bf16[16,64,256]{2,1,0:T(8,128)(2,1)} %get-tuple-element.38), channel_id=1, source_target_pairs={{0,1},{1,0},{2,3},{3,2},{4,5},{5,4},{6,7},{7,6},{8,9},{9,8},{10,11... | collective-permute-start | bytes 1572872 | tf_op jit(solution)/shard_map/ppermute | solution.py:404
  56.2 15.6 %all-to-all-start.2 = ((bf16[32,32,256]{2,1,0:T(8,128)(2,1)}), bf16[32,32,256]{2,1,0:T(8,128)(2,1)S(1)}, u32[]{:S(2)}, u32[]{:S(2)}) async-start(bf16[32,32,256]{2,1,0:T(8,128)(2,1)} %bitcast.58), calls=%async_computation.2 | async-start | bytes 1048576 | tf_op jit(solution)/shard_map/all_to_all | solution.py:407
  61.2 11.9 %copy-start.2 = (bf16[256,256]{1,0:T(8,128)(2,1)S(1)}, bf16[256,256]{1,0:T(8,128)(2,1)}, u32[]{:S(2)}) copy-start(bf16[256,256]{1,0:T(8,128)(2,1)} %get-tuple-element.22.re_ref) | copy-start | bytes 393220
  61.3 11.9 %copy-start.3 = (bf16[256,256]{1,0:T(8,128)(2,1)S(1)}, bf16[256,256]{1,0:T(8,128)(2,1)}, u32[]{:S(2)}) copy-start(bf16[256,256]{1,0:T(8,128)(2,1)} %get-tuple-element.23.im_ref) | copy-start | bytes 393220
  68.6 3.4 %collective-permute-start.5 = (bf16[32,32,256]{2,1,0:T(8,128)(2,1)}, bf16[32,32,256]{2,1,0:T(8,128)(2,1)S(1)}, u32[]{:S(2)}, u32[]{:S(2)}) collective-permute-start(bf16[32,32,256]{2,1,0:T(8,128)(2,1)} %get-tuple-element.28), channel_id=1, source_target_pairs={{0,1},{1,0},{2,3},{3,2},{4,5},{5,4},{6,7},{7,6},{8,9},{9,8},{10,11... | collective-permute-start | bytes 1572872 | tf_op jit(solution)/shard_map/ppermute | solution.py:404
  68.6 3.4 %collective-permute-start.1 = (bf16[32,256]{1,0:T(8,128)(2,1)S(1)}, bf16[32,256]{1,0:T(8,128)(2,1)S(1)}, u32[]{:S(2)}, u32[]{:S(2)}) collective-permute-start(bf16[32,256]{1,0:T(8,128)(2,1)S(1)} %sum_parts.2.u_ref), channel_id=1, source_target_pairs={{0,1},{1,0},{2,3},{3,2},{4,5},{5,4},{6,7},{7,6},{8,9},{9,8},{10,11... | collective-permute-start | bytes 49160 | tf_op jit(solution)/shard_map/ppermute | solution.py:404
  71.9 1.3 %collective-permute-start.4 = (bf16[32,256]{1,0:T(8,128)(2,1)S(1)}, bf16[32,256]{1,0:T(8,128)(2,1)S(1)}, u32[]{:S(2)}, u32[]{:S(2)}) collective-permute-start(bf16[32,256]{1,0:T(8,128)(2,1)S(1)} %sum_parts.3.d_ref), channel_id=1, source_target_pairs={{0,1},{1,0},{2,3},{3,2},{4,5},{5,4},{6,7},{7,6},{8,9},{9,8},{10,11... | collective-permute-start | bytes 49160 | tf_op jit(solution)/shard_map/ppermute | solution.py:404
  106.7 13.8 %collective-permute-start.6 = (bf16[32,32,256]{2,1,0:T(8,128)(2,1)S(1)}, bf16[32,32,256]{2,1,0:T(8,128)(2,1)S(1)}, u32[]{:S(2)}, u32[]{:S(2)}) collective-permute-start(bf16[32,32,256]{2,1,0:T(8,128)(2,1)S(1)} %all_to_all.27), channel_id=1, source_target_pairs={{0,1},{1,0},{2,3},{3,2},{4,5},{5,4},{6,7},{7,6},{8,9},{9,8},{10,11... | collective-permute-start | bytes 1572872 | tf_op jit(solution)/shard_map/ppermute | solution.py:404
  106.8 10.5 %collective-permute-start.7 = (bf16[72,256]{1,0:T(8,128)(2,1)S(1)}, bf16[72,256]{1,0:T(8,128)(2,1)S(1)}, u32[]{:S(2)}, u32[]{:S(2)}) collective-permute-start(bf16[72,256]{1,0:T(8,128)(2,1)S(1)} %get-tuple-element.42), channel_id=1, source_target_pairs={{0,64},{64,128},{128,192},{192,0},{1,65},{65,129},{129,193},{193,1... | collective-permute-start | bytes 110600 | tf_op jit(solution)/shard_map/ppermute | solution.py:453
  110.1 8.3 %collective-permute-start.8 = (bf16[72,256]{1,0:T(8,128)(2,1)S(1)}, bf16[72,256]{1,0:T(8,128)(2,1)S(1)}, u32[]{:S(2)}, u32[]{:S(2)}) collective-permute-start(bf16[72,256]{1,0:T(8,128)(2,1)S(1)} %get-tuple-element.41), channel_id=1, source_target_pairs={{0,128},{64,192},{128,0},{192,64},{1,129},{65,193},{129,1},{193,65... | collective-permute-start | bytes 110600 | tf_op jit(solution)/shard_map/ppermute | solution.py:453
  114.6 5.3 %collective-permute-start.9 = (bf16[72,256]{1,0:T(8,128)(2,1)S(1)}, bf16[72,256]{1,0:T(8,128)(2,1)S(1)}, u32[]{:S(2)}, u32[]{:S(2)}) collective-permute-start(bf16[72,256]{1,0:T(8,128)(2,1)S(1)} %get-tuple-element.40), channel_id=1, source_target_pairs={{0,192},{64,0},{128,64},{192,128},{1,193},{65,1},{129,65},{193,129... | collective-permute-start | bytes 110600 | tf_op jit(solution)/shard_map/ppermute | solution.py:453
  120.6 1.2 copy-start.4

commit v5 on v4

--- a/solution.py
+++ b/solution.py
@@ -67,22 +67,21 @@
         h = dot(inv_ref[...], table).astype(BF)
         hid_ref[b * cols : (b + 1) * cols, :] = h[:cols]
         hid_ref[side + b * cols : side + (b + 1) * cols, :] = h[cols:]
-    for k, ref in ((0, own_ref), (1, par_ref)):
-        rows = slice(k * side, (k + 1) * side)
-        pre_s[k] = dot(hid_ref[rows, :], wi_ref[...])
-        ga_s[k] = dot(ref[...].reshape(side, chan), wot_ref[...])
-        for r in range(0, side, chunk):
-            p = pre_s[k, r : r + chunk, :]
-            g = ga_s[k, r : r + chunk, :]
-            sq = p * p
-            t = 0.5 * jnp.tanh(p * (GELU_A + GELU_B * sq))
-            s = 0.5 + t
-            a = p * s
-            slope = s + (a * (0.5 - t)) * (2.0 * GELU_A + (6.0 * GELU_B) * sq)
-            there = slice(k * side + r, k * side + r + chunk)
-            act_ref[there, :] = a.astype(BF)
-            dpre_ref[there, :] = (g * slope).astype(BF)
-        dh_s[rows, :] = dot(dpre_ref[rows, :], wit_ref[...])
+    flat = (side, chan)
+    cot = jnp.concatenate([own_ref[...].reshape(flat), par_ref[...].reshape(flat)], axis=0)
+    pre_s[...] = dot(hid_ref[...], wi_ref[...])
+    ga_s[...] = dot(cot, wot_ref[...])
+    for r in range(0, 2 * side, chunk):
+        p = pre_s[r : r + chunk, :]
+        g = ga_s[r : r + chunk, :]
+        sq = p * p
+        t = 0.5 * jnp.tanh(p * (GELU_A + GELU_B * sq))
+        s = 0.5 + t
+        a = p * s
+        slope = s + (a * (0.5 - t)) * (2.0 * GELU_A + (6.0 * GELU_B) * sq)
+        act_ref[r : r + chunk, :] = a.astype(BF)
+        dpre_ref[r : r + chunk, :] = (g * slope).astype(BF)
+    dh_s[...] = dot(dpre_ref[...], wit_ref[...])
     for b in range(block):
         lines = pl.ds(i * block + b, modes, stride=half)
         mine = dh_s[b * cols : (b + 1) * cols, :]
@@ -131,7 +130,7 @@
             pltpu.HBM((modes * half, chan), BF),
         ],
         scratch_shapes=[pltpu.VMEM((modes * half, LANES), F32)] * 4
-        + [pltpu.VMEM((2, block * cols, width), F32)] * 2
+        + [pltpu.VMEM((rows, width), F32)] * 2
         + [pltpu.VMEM((rows, chan), F32)],
         compiler_params=pltpu.CompilerParams(vmem_limit_bytes=30 << 20),
         name="mlp",
@@ -207,7 +206,7 @@
             jax.ShapeDtypeStruct((chips, kept, chan), F32),
             jax.ShapeDtypeStruct((chips, kept, chan), BF),
         ],
-        compiler_params=pltpu.CompilerParams(vmem_limit_bytes=26 << 20),
+        compiler_params=pltpu.CompilerParams(vmem_limit_bytes=34 << 20),
         name="grads",
     )(core.reshape(1), in_hbm(hidden), in_hbm(d_pre), in_hbm(act), own, par)
 

time: 125 us -> 124 us (level)
  no operation moved by 1% of the time
where the time goes in v5:
time: 124 us; the launch traced here: 123 us
  blocking collectives  54.6 us (44%)
  starting transfers between devices  21.5 us (17%)
  Pallas kernels  20.3 us (16%)
  waiting for transfers between devices  15 us (12%)
  local copies, waits for them, and re-layouts  7.62 us (6%)
  other arithmetic  1.83 us (1%)
  matrix products  1.24 us (1%)
    all_to_all x3, blocking collectives, spread(): return lax.all_to_all(x, 'gx', 0, 0, tiled=True, axis_index_groups=groups)  54.6 us
    ppermute x3, starting transfers between devices, local(): lax.ppermute(sent, 'gy', [(i, (i + d) % ny) for i in range(ny)])  10.7 us
    pallas_call x1, Pallas kernels, mlp_call(): pl.pallas_call(mlp_kernel, grid=(half // block,), in_specs=[pl.BlockSpec(...  10.6 us
    all_to_all x2, starting transfers between devices, spread(): return lax.all_to_all(x, 'gx', 0, 0, tiled=True, axis_index_groups=groups)  10 us
    all_to_all x2, waiting for transfers between devices, spread(): return lax.all_to_all(x, 'gx', 0, 0, tiled=True, axis_index_groups=groups)  9.7 us
    pallas_call x1, Pallas kernels, grads_call(): pl.pallas_call(grads_kernel, grid_spec=pltpu.PrefetchScalarGridSpec(num_s...  7.31 us
    unnamed x12, local copies, waits for them, and re-layouts  4.01 us
    ppermute x7, waiting for transfers between devices, pair(): return lax.ppermute(x, 'gx', swap)  2.74 us
  transfers between devices with their start and end apart: 12, of which 7 were waited for; matrix products, arithmetic and copies ran while one was open for 5% of the time, Pallas kernels for 7%

profile of v5, /device:TPU:2, one launch (start us, length us, event | category | flops | bytes accessed | tf_op | source)
XLA Modules:
  0.0 123.1 jit_solution(6528581571945799031)
XLA Ops:
  0.6 0.0 copy-start
  0.7 1.2 copy-done
  1.9 0.1 collective-permute-start
  2.0 0.2 multiply_convert_fusion.3
  2.3 1.0 copy.32
  3.3 0.3 fusion.2
  3.6 0.3 collective-permute-done
  3.9 0.3 fusion.1
  4.2 0.3 copy.31
  4.6 21.5 %all_to_all.25.recv_ref = bf16[32,40,256]{2,1,0:T(8,128)(2,1)S(1)} all-to-all(bf16[32,40,256]{2,1,0:T(8,128)(2,1)S(1)} %pad_maximum_fusion), channel_id=1, replica_groups={{0,2,4,6,8,10,12,14,16,18,20,22,24,26,28,30,32,34,36,38,40,42,44,46,48,..., dimensions={0} | all-to-all | bytes 1310720 | tf_op jit(solution)/shard_map/all_to_all | solution.py:406
  26.1 0.0 copy-start.1
  26.1 0.1 collective-permute-start.2
  26.2 0.1 sum_parts.2.u_ref
  26.3 1.3 %collective-permute-done.2.par_ref = bf16[32,8,256]{2,1,0:T(8,128)(2,1)S(1)} collective-permute-done((bf16[32,8,256]{2,1,0:T(8,128)(2,1)S(1)}, bf16[32,8,256]{2,1,0:T(8,128)(2,1)S(1)}, u32[]{:S(2)}, u32[]{:S(2)}) %collective-permute-start.2) | collective-permute-done | bytes 131104 | tf_op jit(solution)/shard_map/ppermute | solution.py:403
  27.5 1.1 mix.1
  28.6 5.0 %all-to-all-start.1 = ((bf16[32,32,256]{2,1,0:T(8,128)(2,1)}), bf16[32,32,256]{2,1,0:T(8,128)(2,1)S(1)}, u32[]{:S(2)}, u32[]{:S(2)}) async-start(bf16[32,32,256]{2,1,0:T(8,128)(2,1)} %get-tuple-element.20), calls=%async_computation.1 | async-start | bytes 1048576 | tf_op jit(solution)/shard_map/all_to_all | solution.py:406
  33.6 2.1 %dynamic-slice_bitcast_fusion = (bf16[16,64,256]{2,1,0:T(8,128)(2,1)}, bf16[16,64,256]{2,1,0:T(8,128)(2,1)S(1)}) fusion(bf16[2,16,64,256]{3,2,1,0:T(8,128)(2,1)} %bitcast.53, s32[]{:T(128)S(6)} %select_n.118, s32[]{:T(128)S(6)} %select_n.116), kind=kLoop, calls=%fused_computation.11 | loop fusion | bytes 2097160 | tf_op jit(solution)/shard_map/jit(dynamic_index_in_dim)/squeeze | solution.py:409
  35.7 0.0 collective-permute-start.3
  35.8 0.1 pad_maximum_fusion.5
  35.8 0.1 copy.37.inv_ref
  36.0 0.2 copy.35
  36.2 2.0 %copy.36 = bf16[1024,256]{0,1:T(8,128)(2,1)} copy(bf16[1024,256]{1,0:T(8,128)(2,1)} %param.9) | data formatting | bytes 1048576 | tf_op args[4]
  38.2 0.1 fusion.29.invt_ref
  38.3 7.0 %all-to-all-done.1 = bf16[32,32,256]{2,1,0:T(8,128)(2,1)S(1)} async-done(((bf16[32,32,256]{2,1,0:T(8,128)(2,1)}), bf16[32,32,256]{2,1,0:T(8,128)(2,1)S(1)}, u32[]{:S(2)}, u32[]{:S(2)}) %all-to-all-start.1) | async-done | bytes 524320 | tf_op jit(solution)/shard_map/all_to_all | solution.py:406
  45.3 10.6 %mlp.1 = (bf16[2048,256]{1,0:T(8,128)(2,1)}, bf16[2048,1024]{1,0:T(8,128)(2,1)}, bf16[2048,1024]{1,0:T(8,128)(2,1)}, bf16[1024,256]{1,0:T(8,128)(2,1)}) custom-call(bf16[1024,256]{1,0:T(8,128)(2,1)S(1)} %bitcast.51, bf16[16,64,256]{2,1,0:T(8,128)(2,1)S(1)} %get-tuple-element.39.own_ref, bf16[16,64,256]{2,1,0:T(8,128)(2,1)} %collective-permute-done.3.par_ref, ...), custom_call_target="tpu_custom_call" | custom-call | tf_op jit(solution)/shard_map/mlp/pallas_call | solution.py:107
  55.9 5.0 %all-to-all-start.2 = ((bf16[32,32,256]{2,1,0:T(8,128)(2,1)}), bf16[32,32,256]{2,1,0:T(8,128)(2,1)S(1)}, u32[]{:S(2)}, u32[]{:S(2)}) async-start(bf16[32,32,256]{2,1,0:T(8,128)(2,1)} %bitcast.58), calls=%async_computation.2 | async-start | bytes 1048576 | tf_op jit(solution)/shard_map/all_to_all | solution.py:406
  61.0 7.3 %grads.1 = (f32[32,32,256]{2,1,0:T(8,128)S(1)}, bf16[32,32,256]{2,1,0:T(8,128)(2,1)}) custom-call(s32[1]{0:T(128)} %bitcast.2.core_ref, bf16[2048,256]{1,0:T(8,128)(2,1)} %get-tuple-element.24.hid_ref, bf16[2048,1024]{1,0:T(8,128)(2,1)} %get-tuple-element.25.dpre_ref, bf16[2048,1024]{1,0:T(8,128)(2,1)} %get-tuple-element.26.act_ref, ...), custom_call_target="tpu_custom_call" | custom-call | tf_op jit(solution)/shard_map/grads/pallas_call | solution.py:187
  68.3 0.5 collective-permute-start.1
  68.8 2.7 %all-to-all-done.2.recv_ref = bf16[32,32,256]{2,1,0:T(8,128)(2,1)S(1)} async-done(((bf16[32,32,256]{2,1,0:T(8,128)(2,1)}), bf16[32,32,256]{2,1,0:T(8,128)(2,1)S(1)}, u32[]{:S(2)}, u32[]{:S(2)}) %all-to-all-start.2) | async-done | bytes 524320 | tf_op jit(solution)/shard_map/all_to_all | solution.py:406
  71.5 0.1 sum_parts.3.d_ref
  71.6 0.1 collective-permute-start.4
  71.7 1.1 collective-permute-done.4.dpar_ref
  72.9 0.4 last.1
  73.3 18.5 %all_to_all.26.recv_ref = bf16[32,40,256]{2,1,0:T(8,128)(2,1)S(1)} all-to-all(bf16[32,40,256]{2,1,0:T(8,128)(2,1)S(1)} %get-tuple-element.29), channel_id=1, replica_groups={{0,2,4,6,8,10,12,14,16,18,20,22,24,26,28,30,32,34,36,38,40,42,44,46,48,..., dimensions={0} | all-to-all | bytes 1310720 | tf_op jit(solution)/shard_map/all_to_all | solution.py:406
  91.8 14.6 %all_to_all.27 = bf16[32,32,256]{2,1,0:T(8,128)(2,1)S(1)} all-to-all(bf16[32,32,256]{2,1,0:T(8,128)(2,1)S(1)} %get-tuple-element.31), channel_id=1, replica_groups={{0,2,4,6,8,10,12,14,16,18,20,22,24,26,28,30,32,34,36,38,40,42,44,46,48,..., dimensions={0} | all-to-all | bytes 1048576 | tf_op jit(solution)/shard_map/all_to_all | solution.py:406
  106.4 0.1 lines_rows.1.blocks_ref
  106.5 3.5 %collective-permute-start.7 = (bf16[72,256]{1,0:T(8,128)(2,1)S(1)}, bf16[72,256]{1,0:T(8,128)(2,1)S(1)}, u32[]{:S(2)}, u32[]{:S(2)}) collective-permute-start(bf16[72,256]{1,0:T(8,128)(2,1)S(1)} %get-tuple-element.42), channel_id=1, source_target_pairs={{0,64},{64,128},{128,192},{192,0},{1,65},{65,129},{129,193},{193,1... | collective-permute-start | bytes 110600 | tf_op jit(solution)/shard_map/ppermute | solution.py:452
  110.0 4.5 %collective-permute-start.8 = (bf16[72,256]{1,0:T(8,128)(2,1)S(1)}, bf16[72,256]{1,0:T(8,128)(2,1)S(1)}, u32[]{:S(2)}, u32[]{:S(2)}) collective-permute-start(bf16[72,256]{1,0:T(8,128)(2,1)S(1)} %get-tuple-element.41), channel_id=1, source_target_pairs={{0,128},{64,192},{128,0},{192,64},{1,129},{65,193},{129,1},{193,65... | collective-permute-start | bytes 110600 | tf_op jit(solution)/shard_map/ppermute | solution.py:452
  114.5 2.7 %collective-permute-start.9 = (bf16[72,256]{1,0:T(8,128)(2,1)S(1)}, bf16[72,256]{1,0:T(8,128)(2,1)S(1)}, u32[]{:S(2)}, u32[]{:S(2)}) collective-permute-start(bf16[72,256]{1,0:T(8,128)(2,1)S(1)} %get-tuple-element.40), channel_id=1, source_target_pairs={{0,192},{64,0},{128,64},{192,128},{1,193},{65,1},{129,65},{193,129... | collective-permute-start | bytes 110600 | tf_op jit(solution)/shard_map/ppermute | solution.py:452
  117.2 1.2 collective-permute-done.8.two_ref
  118.4 1.4 %collective-permute-done.9.three_ref = bf16[72,256]{1,0:T(8,128)(2,1)S(1)} collective-permute-done((bf16[72,256]{1,0:T(8,128)(2,1)S(1)}, bf16[72,256]{1,0:T(8,128)(2,1)S(1)}, u32[]{:S(2)}, u32[]{:S(2)}) %collective-permute-start.9) | collective-permute-done | bytes 36896 | tf_op jit(solution)/shard_map/ppermute | solution.py:452
  119.8 0.7 final.1
  120.4 0.1 broadcast_select_fusion.1
  120.5 0.0 copy-start.4
  120.5 0.3 convolution_bitcast_fusion.1
  120.8 0.3 convolution_bitcast_fusion
  121.2 0.5 copy-done.4
  121.7 1.4 %fusion = bf16[32,64,256]{2,1,0:T(8,128)(2,1)} fusion(f32[16,64,256]{2,1,0:T(8,128)S(1)} %convolution_bitcast_fusion, f32[16,64,256]{2,1,0:T(8,128)S(1)} %convolution_bitcast_fusion.1, bf16[32,64,256]{2,1,0:T(8,128)(2,1)S(1)} %copy-done.4), kind=kLoop, calls=%fused_computation.1 | loop fusion | flops 2097152 | bytes 4194304 | tf_op jit(solution)/shard_map/convert_element_type | solution.py:460
  (28 shorter events, 0.3 us)
Async XLA Ops:
  0.6 1.2 %copy-start = (bf16[32,64,256]{2,1,0:T(8,128)(2,1)S(1)}, bf16[32,64,256]{2,1,0:T(8,128)(2,1)}, u32[]{:S(2)}) copy-start(bf16[32,64,256]{2,1,0:T(8,128)(2,1)} %param.5) | copy-start | bytes 3145732
  1.9 2.0 %collective-permute-start = (bf16[16,64,256]{2,1,0:T(8,128)(2,1)S(1)}, bf16[16,64,256]{2,1,0:T(8,128)(2,1)S(1)}, u32[]{:S(2)}, u32[]{:S(2)}) collective-permute-start(bf16[16,64,256]{2,1,0:T(8,128)(2,1)S(1)} %dynamic-slice_bitcast_fusion.2), channel_id=1, source_target_pairs={{0,1},{1,0},{2,3},{3,2},{4,5},{5,4},{6,7},{7,6},{8,9},{9,8},{10,11... | collective-permute-start | bytes 1572872 | tf_op jit(solution)/shard_map/ppermute | solution.py:403
  26.1 9.9 %copy-start.1 = (bf16[256,1024]{1,0:T(8,128)(2,1)S(1)}, bf16[256,1024]{1,0:T(8,128)(2,1)}, u32[]{:S(2)}) copy-start(bf16[256,1024]{1,0:T(8,128)(2,1)} %wi_ref.1) | copy-start | bytes 1572868
  26.1 1.4 %collective-permute-start.2 = (bf16[32,8,256]{2,1,0:T(8,128)(2,1)S(1)}, bf16[32,8,256]{2,1,0:T(8,128)(2,1)S(1)}, u32[]{:S(2)}, u32[]{:S(2)}) collective-permute-start(bf16[32,8,256]{2,1,0:T(8,128)(2,1)S(1)} %slice.4.own_ref), channel_id=1, source_target_pairs={{0,1},{1,0},{2,3},{3,2},{4,5},{5,4},{6,7},{7,6},{8,9},{9,8},{10,11... | collective-permute-start | bytes 393224 | tf_op jit(solution)/shard_map/ppermute | solution.py:403
  28.6 16.7 %all-to-all-start.1 = ((bf16[32,32,256]{2,1,0:T(8,128)(2,1)}), bf16[32,32,256]{2,1,0:T(8,128)(2,1)S(1)}, u32[]{:S(2)}, u32[]{:S(2)}) async-start(bf16[32,32,256]{2,1,0:T(8,128)(2,1)} %get-tuple-element.20), calls=%async_computation.1 | async-start | bytes 1048576 | tf_op jit(solution)/shard_map/all_to_all | solution.py:406
  35.7 2.6 %collective-permute-start.3 = (bf16[16,64,256]{2,1,0:T(8,128)(2,1)}, bf16[16,64,256]{2,1,0:T(8,128)(2,1)}, u32[]{:S(2)}, u32[]{:S(2)}) collective-permute-start(bf16[16,64,256]{2,1,0:T(8,128)(2,1)} %get-tuple-element.38), channel_id=1, source_target_pairs={{0,1},{1,0},{2,3},{3,2},{4,5},{5,4},{6,7},{7,6},{8,9},{9,8},{10,11... | collective-permute-start | bytes 1572872 | tf_op jit(solution)/shard_map/ppermute | solution.py:403
  55.9 15.6 %all-to-all-start.2 = ((bf16[32,32,256]{2,1,0:T(8,128)(2,1)}), bf16[32,32,256]{2,1,0:T(8,128)(2,1)S(1)}, u32[]{:S(2)}, u32[]{:S(2)}) async-start(bf16[32,32,256]{2,1,0:T(8,128)(2,1)} %bitcast.58), calls=%async_computation.2 | async-start | bytes 1048576 | tf_op jit(solution)/shard_map/all_to_all | solution.py:406
  60.9 11.9 %copy-start.2 = (bf16[256,256]{1,0:T(8,128)(2,1)S(1)}, bf16[256,256]{1,0:T(8,128)(2,1)}, u32[]{:S(2)}) copy-start(bf16[256,256]{1,0:T(8,128)(2,1)} %get-tuple-element.22.re_ref) | copy-start | bytes 393220
  61.0 11.9 %copy-start.3 = (bf16[256,256]{1,0:T(8,128)(2,1)S(1)}, bf16[256,256]{1,0:T(8,128)(2,1)}, u32[]{:S(2)}) copy-start(bf16[256,256]{1,0:T(8,128)(2,1)} %get-tuple-element.23.im_ref) | copy-start | bytes 393220
  68.3 3.4 %collective-permute-start.5 = (bf16[32,32,256]{2,1,0:T(8,128)(2,1)}, bf16[32,32,256]{2,1,0:T(8,128)(2,1)S(1)}, u32[]{:S(2)}, u32[]{:S(2)}) collective-permute-start(bf16[32,32,256]{2,1,0:T(8,128)(2,1)} %get-tuple-element.28), channel_id=1, source_target_pairs={{0,1},{1,0},{2,3},{3,2},{4,5},{5,4},{6,7},{7,6},{8,9},{9,8},{10,11... | collective-permute-start | bytes 1572872 | tf_op jit(solution)/shard_map/ppermute | solution.py:403
  68.3 3.4 %collective-permute-start.1 = (bf16[32,256]{1,0:T(8,128)(2,1)S(1)}, bf16[32,256]{1,0:T(8,128)(2,1)S(1)}, u32[]{:S(2)}, u32[]{:S(2)}) collective-permute-start(bf16[32,256]{1,0:T(8,128)(2,1)S(1)} %sum_parts.2.u_ref), channel_id=1, source_target_pairs={{0,1},{1,0},{2,3},{3,2},{4,5},{5,4},{6,7},{7,6},{8,9},{9,8},{10,11... | collective-permute-start | bytes 49160 | tf_op jit(solution)/shard_map/ppermute | solution.py:403
  71.6 1.3 %collective-permute-start.4 = (bf16[32,256]{1,0:T(8,128)(2,1)S(1)}, bf16[32,256]{1,0:T(8,128)(2,1)S(1)}, u32[]{:S(2)}, u32[]{:S(2)}) collective-permute-start(bf16[32,256]{1,0:T(8,128)(2,1)S(1)} %sum_parts.3.d_ref), channel_id=1, source_target_pairs={{0,1},{1,0},{2,3},{3,2},{4,5},{5,4},{6,7},{7,6},{8,9},{9,8},{10,11... | collective-permute-start | bytes 49160 | tf_op jit(solution)/shard_map/ppermute | solution.py:403
  106.4 14.0 %collective-permute-start.6 = (bf16[32,32,256]{2,1,0:T(8,128)(2,1)S(1)}, bf16[32,32,256]{2,1,0:T(8,128)(2,1)S(1)}, u32[]{:S(2)}, u32[]{:S(2)}) collective-permute-start(bf16[32,32,256]{2,1,0:T(8,128)(2,1)S(1)} %all_to_all.27), channel_id=1, source_target_pairs={{0,1},{1,0},{2,3},{3,2},{4,5},{5,4},{6,7},{7,6},{8,9},{9,8},{10,11... | collective-permute-start | bytes 1572872 | tf_op jit(solution)/shard_map/ppermute | solution.py:403
  106.5 10.7 %collective-permute-start.7 = (bf16[72,256]{1,0:T(8,128)(2,1)S(1)}, bf16[72,256]{1,0:T(8,128)(2,1)S(1)}, u32[]{:S(2)}, u32[]{:S(2)}) collective-permute-start(bf16[72,256]{1,0:T(8,128)(2,1)S(1)} %get-tuple-element.42), channel_id=1, source_target_pairs={{0,64},{64,128},{128,192},{192,0},{1,65},{65,129},{129,193},{193,1... | collective-permute-start | bytes 110600 | tf_op jit(solution)/shard_map/ppermute | solution.py:452
  110.0 8.3 %collective-permute-start.8 = (bf16[72,256]{1,0:T(8,128)(2,1)S(1)}, bf16[72,256]{1,0:T(8,128)(2,1)S(1)}, u32[]{:S(2)}, u32[]{:S(2)}) collective-permute-start(bf16[72,256]{1,0:T(8,128)(2,1)S(1)} %get-tuple-element.41), channel_id=1, source_target_pairs={{0,128},{64,192},{128,0},{192,64},{1,129},{65,193},{129,1},{193,65... | collective-permute-start | bytes 110600 | tf_op jit(solution)/shard_map/ppermute | solution.py:452
  114.5 5.3 %collective-permute-start.9 = (bf16[72,256]{1,0:T(8,128)(2,1)S(1)}, bf16[72,256]{1,0:T(8,128)(2,1)S(1)}, u32[]{:S(2)}, u32[]{:S(2)}) collective-permute-start(bf16[72,256]{1,0:T(8,128)(2,1)S(1)} %get-tuple-element.40), channel_id=1, source_target_pairs={{0,192},{64,0},{128,64},{192,128},{1,193},{65,1},{129,65},{193,129... | collective-permute-start | bytes 110600 | tf_op jit(solution)/shard_map/ppermute | solution.py:452
  120.5 1.2 copy-start.4
